TPU v7x, 32 devices: a whole 2x2x4 slice. The times are simulated.
32 devices in a mesh: ctx: 8 (over z, x), fsdp: 4 (over y, core).
Axes of the slice: x: 2, y: 2, z: 4, core: 2. Of those that a mesh axis runs over, the one named last changes fastest.
Arguments:
- inputs: bfloat16 [4, 1024, 1024], P('fsdp', 'ctx'), may hold values from -6 to 6
- segment_ids: int32 [4, 1024], P('fsdp', 'ctx'), may hold values from 0 to 1, never falling along the last dimension, each value on 1 to 768 neighbouring positions
- gain_attn: bfloat16 [1024], P(('ctx', 'fsdp')), may hold values from 0.5 to 1.5
- w_qkv: bfloat16 [1024, 3072], P(('ctx', 'fsdp')), may hold values from -4 to 4
- w_out_attn: bfloat16 [1024, 1024], P(('ctx', 'fsdp')), may hold values from -1.5 to 1.5
- gain_mlp: bfloat16 [1024], P(('ctx', 'fsdp')), may hold values from 0.5 to 1.5
- w_in: bfloat16 [1024, 5248], P(('ctx', 'fsdp')), may hold values from -0.1875 to 0.1875
- w_out_mlp: bfloat16 [2624, 1024], P(None, ('ctx', 'fsdp')), may hold values from -0.125 to 0.125
- cotangent: bfloat16 [4, 1024, 1024], P('fsdp', 'ctx'), may hold values from -6 to 6
Outputs:
- block_out: bfloat16 [4, 1024, 1024], P('fsdp', 'ctx')
- grad_input: bfloat16 [4, 1024, 1024], P('fsdp', 'ctx')
- grad_w_qkv: float32 [1024, 3072], P(('ctx', 'fsdp'))
- grad_w_out_attn: float32 [1024, 1024], P(('ctx', 'fsdp'))
- grad_w_in: float32 [1024, 5248], P(('ctx', 'fsdp'))
- grad_w_out_mlp: float32 [2624, 1024], P(None, ('ctx', 'fsdp'))
- grad_gain_attn: float32 [1024], P(('ctx', 'fsdp'))
- grad_gain_mlp: float32 [1024], P(('ctx', 'fsdp'))
Inputs may be any that keep to these rules, and one draw needn't show every extreme that they name: `segment_ids`: along a row the ids never fall: segment 0 comes first, then segment 1; each segment holds 256 to 768 tokens.
All inputs are finite; a program needn't handle non-finite values.
Results may differ from a plain program's by a relative error of at most 0.015.
Values may be sent and summed in bfloat16 or wider, within the bound.
A program may use at most 256 MiB of HBM per device.

v0:
```python
import functools
import math

import jax
import jax.numpy as jnp
from jax import lax
from jax.experimental import pallas as pl
from jax.experimental.pallas import tpu as pltpu
from jax.sharding import PartitionSpec as P

HEADS = 16
HD = 64


EPSILON = 1e-05
ROPE_BASE = 160000.0
MASKED = -1e30


def layer_norm(values):
    center = values - jnp.mean(values, axis=-1, keepdims=True)
    scaled = lax.rsqrt(jnp.mean(center * center, axis=-1, keepdims=True) + EPSILON)
    return (center * scaled, scaled)


def norm_back(grad_norm, normed, scaled):
    return scaled * (
        grad_norm
        - jnp.mean(grad_norm, axis=-1, keepdims=True)
        - normed * jnp.mean(grad_norm * normed, axis=-1, keepdims=True)
    )


def rope_columns(positions, head_size):
    freqs = ROPE_BASE ** (-jnp.arange(0, head_size, 2, dtype=jnp.float32) / head_size)
    angles = freqs[:, None] * positions[None, :]
    cosine = jnp.concatenate([jnp.cos(angles), jnp.cos(angles)], axis=0)
    sine = jnp.concatenate([jnp.sin(angles), jnp.sin(angles)], axis=0)
    return (cosine[None], sine[None])


def rotate_cols(values, cosine, sine):
    half = values.shape[1] // 2
    turned = jnp.concatenate([-values[:, half:], values[:, :half]], axis=1)
    return values * cosine + turned * sine


def unrotate_cols(grads, cosine, sine):
    half = grads.shape[1] // 2
    weighted = grads * sine
    turned = jnp.concatenate([weighted[:, half:], -weighted[:, :half]], axis=1)
    return grads * cosine + turned


def gelu_slope(values):
    return (
        0.5 * (1.0 + lax.erf(values * 0.7071067811865476))
        + values * jnp.exp(-0.5 * values * values) * 0.3989422804014327
    )


LANES = 128
SEG_ROWS = 16
QUERY_BLOCK = 256


def masked_scores(query, key, same, scale):
    scores = lax.dot_general(query, key, (((0,), (0,)), ((), ())), preferred_element_type=jnp.float32)
    return jnp.where(same, scores * scale, MASKED)


def attend_kernel(scale, query_ref, key_ref, value_ref, seg_own_ref, seg_ref, out_ref, log_ref):
    same = seg_own_ref[...] == seg_ref[...]
    scores = masked_scores(query_ref[0], key_ref[0], same, scale)
    peak = jnp.max(scores, axis=-1, keepdims=True)
    log_total = peak + jnp.log(jnp.sum(jnp.exp(scores - peak), axis=-1, keepdims=True))
    log_ref[0] = log_total
    probs = jnp.exp(scores - log_total).astype(jnp.bfloat16)
    out_ref[0] = lax.dot_general(
        value_ref[0], probs, (((1,), (1,)), ((), ())), preferred_element_type=jnp.float32
    ).astype(jnp.bfloat16)


def attend_grad_kernel(
    scale,
    query_ref,
    key_ref,
    value_ref,
    seg_own_ref,
    seg_ref,
    log_ref,
    grad_ref,
    attended_ref,
    query_grad_ref,
    key_grad_ref,
    value_grad_ref,
):
    @pl.when(pl.program_id(1) == 0)
    def _():
        key_grad_ref[...] = jnp.zeros_like(key_grad_ref)
        value_grad_ref[...] = jnp.zeros_like(value_grad_ref)

    query = query_ref[0]
    grad = grad_ref[0]
    key = key_ref[0]
    dots_row = jnp.sum(
        grad.astype(jnp.float32) * attended_ref[0].astype(jnp.float32), axis=0, keepdims=True
    )
    dots = jnp.transpose(jnp.broadcast_to(dots_row, (8, dots_row.shape[1])))[:, :1]
    same = seg_own_ref[...] == seg_ref[...]
    probs = jnp.exp(masked_scores(query, key, same, scale) - log_ref[0])
    grad_probs = lax.dot_general(
        grad, value_ref[0], (((0,), (0,)), ((), ())), preferred_element_type=jnp.float32
    )
    grad_scores = (probs * (grad_probs - dots)).astype(jnp.bfloat16)
    query_grad_ref[0] = scale * lax.dot_general(
        key, grad_scores, (((1,), (1,)), ((), ())), preferred_element_type=jnp.float32
    )
    key_grad_ref[0] += scale * lax.dot_general(
        query, grad_scores, (((1,), (0,)), ((), ())), preferred_element_type=jnp.float32
    )
    value_grad_ref[0] += lax.dot_general(
        grad, probs.astype(jnp.bfloat16), (((1,), (0,)), ((), ())), preferred_element_type=jnp.float32
    )


def attention_specs(head_size, row_count, block):
    part = pl.BlockSpec((1, head_size, block), lambda h, b: (h, 0, b))
    full = pl.BlockSpec((1, head_size, row_count), lambda h, b: (h, 0, 0))
    seg_own = pl.BlockSpec((block, 1), lambda h, b: (b, 0))
    seg_all = pl.BlockSpec((1, row_count), lambda h, b: (0, 0))
    log = pl.BlockSpec((1, block, 1), lambda h, b: (h, b, 0))
    return part, full, seg_own, seg_all, log


def attend(query_cols, key_cols, value_cols, seg_col, seg_row, scale):
    heads, head_size, row_count = query_cols.shape
    block = min(QUERY_BLOCK, row_count)
    part, full, own, every, log = attention_specs(head_size, row_count, block)
    return pl.pallas_call(
        lambda *refs: attend_kernel(scale, *refs),
        grid=(heads, row_count // block),
        in_specs=[part, full, full, own, every],
        out_specs=[part, log],
        out_shape=[
            jax.ShapeDtypeStruct((heads, head_size, row_count), jnp.bfloat16),
            jax.ShapeDtypeStruct((heads, row_count, 1), jnp.float32),
        ],
        name="attend",
    )(query_cols, key_cols, value_cols, seg_col, seg_row)


def attend_grads(
    query_cols, key_cols, value_cols, seg_col, seg_row, log_total, grad_cols, attended_cols, scale
):
    heads, head_size, row_count = query_cols.shape
    block = min(QUERY_BLOCK, row_count)
    part, full, own, every, log = attention_specs(head_size, row_count, block)
    grads = jax.ShapeDtypeStruct((heads, head_size, row_count), jnp.float32)
    return pl.pallas_call(
        lambda *refs: attend_grad_kernel(scale, *refs),
        grid=(heads, row_count // block),
        in_specs=[part, full, full, own, every, log, part, part],
        out_specs=[part, full, full],
        out_shape=[grads, grads, grads],
        name="attend_grads",
    )(query_cols, key_cols, value_cols, seg_col, seg_row, log_total, grad_cols, attended_cols)


def weight_grads_kernel(bounds, *refs):
    gain_ref, out_ref = refs[-2:]
    for i in range(3):
        out_ref[:, bounds[i] : bounds[i] + refs[2 * i + 1].shape[1]] = lax.dot_general(
            refs[2 * i][...],
            refs[2 * i + 1][...],
            (((0,), (0,)), ((), ())),
            preferred_element_type=jnp.float32,
        ).astype(jnp.bfloat16)
    out_ref[:, bounds[3] : bounds[3] + LANES] = gain_ref[...]


def weight_grads(pairs, gain_block, bounds, total):
    tok_count, width = pairs[0][0].shape
    rows = min(LANES, width)
    in_specs = []
    operands = []
    for left, right in pairs:
        in_specs.append(pl.BlockSpec((tok_count, rows), lambda r: (0, r)))
        in_specs.append(pl.BlockSpec(right.shape, lambda r: (0, 0)))
        operands += [left, right]
    in_specs.append(pl.BlockSpec((rows, LANES), lambda r: (r, 0)))
    return pl.pallas_call(
        lambda *refs: weight_grads_kernel(bounds, *refs),
        grid=(width // rows,),
        in_specs=in_specs,
        out_specs=pl.BlockSpec((rows, total), lambda r: (r, 0)),
        out_shape=jax.ShapeDtypeStruct((width, total), jnp.bfloat16),
        name="weight_grads",
    )(*operands, gain_block)


def body(
    ctx_size,
    fsdp_size,
    inputs,
    segment_ids,
    gain_attn,
    w_qkv,
    w_out_attn,
    gain_mlp,
    w_in,
    w_out_mlp,
    cotangent,
):
    tok_count, width = inputs.shape[1:]
    heads = HEADS
    head_size = HD
    scale = 1.0 / math.sqrt(head_size)
    everyone = ("ctx", "fsdp")
    hidden_units = w_out_mlp.shape[0]
    row_count = ctx_size * tok_count
    devices = ctx_size * fsdp_size
    own_heads = heads // ctx_size
    own_width = own_heads * head_size
    weight_rows = w_qkv.shape[0]

    seg_block = jnp.pad(segment_ids.astype(jnp.bfloat16), ((0, SEG_ROWS - 1), (0, width - tok_count)))
    gathered = lax.all_to_all(
        jnp.broadcast_to(
            jnp.concatenate([inputs[0], seg_block], axis=0),
            (ctx_size, tok_count + SEG_ROWS, width),
        ),
        "ctx",
        0,
        0,
        tiled=True,
    )

    qkv_parts = jnp.transpose(
        w_qkv.reshape(weight_rows, 3, ctx_size, own_width), (2, 0, 1, 3)
    ).reshape(ctx_size, weight_rows, 3 * own_width)
    gains_own = jnp.pad(jnp.stack([gain_attn, gain_mlp], axis=1), ((0, 0), (0, LANES - 2)))
    qkv_parts = jnp.concatenate(
        [qkv_parts, jnp.broadcast_to(gains_own, (ctx_size, weight_rows, LANES))], axis=2
    )
    qkv_parts = jnp.broadcast_to(
        qkv_parts[:, None], (ctx_size, fsdp_size, weight_rows, 3 * own_width + LANES)
    ).reshape(devices, weight_rows, 3 * own_width + LANES)
    qkv_got = lax.all_to_all(qkv_parts, everyone, 0, 0, tiled=True).reshape(
        devices * weight_rows, 3 * own_width + LANES
    )
    qkv_mine = qkv_got[:, : 3 * own_width]
    gains = qkv_got[:, 3 * own_width : 3 * own_width + 2].astype(jnp.float32).T
    gain_first = gains[0]
    gain_second = gains[1]

    rest_own = jnp.concatenate([w_out_attn, w_in, w_out_mlp.T], axis=1)
    rest_full = lax.all_gather(rest_own, everyone, axis=0, tiled=True)
    attn_full = rest_full[:, :width]
    in_full = rest_full[:, width : width + 2 * hidden_units]
    mlp_turned = rest_full[:, width + 2 * hidden_units :]

    seg_row = gathered[:, tok_count, :tok_count].reshape(1, row_count).astype(jnp.float32)
    seg_col = seg_row.reshape(row_count, 1)
    row_tokens = gathered[:, :tok_count].reshape(row_count, width).astype(jnp.float32)
    row_normed, unused = layer_norm(row_tokens)
    row_normed_attn = (row_normed * gain_first).astype(jnp.bfloat16)
    tokens = inputs[0].astype(jnp.float32)
    normed_one, scale_one = layer_norm(tokens)

    projected_cols = jnp.einsum(
        "de,td->et", qkv_mine, row_normed_attn, preferred_element_type=jnp.float32
    ).reshape(3, own_heads, head_size, row_count)
    positions = jnp.arange(row_count, dtype=jnp.int32).astype(jnp.float32)
    cosine, sine = rope_columns(positions, head_size)
    query_cols = rotate_cols(projected_cols[0], cosine, sine).astype(jnp.bfloat16)
    key_cols = rotate_cols(projected_cols[1], cosine, sine).astype(jnp.bfloat16)
    value_cols = projected_cols[2].astype(jnp.bfloat16)
    row_attended, log_total = attend(query_cols, key_cols, value_cols, seg_col, seg_row, scale)

    attended = lax.all_to_all(
        row_attended.reshape(own_width, row_count).T.reshape(ctx_size, tok_count, own_width),
        "ctx",
        0,
        0,
        tiled=True,
    )
    attended = jnp.transpose(attended, (1, 0, 2)).reshape(tok_count, width)
    residual = tokens + jnp.dot(attended, attn_full, preferred_element_type=jnp.float32)
    normed_two, scale_two = layer_norm(residual)
    normed_mlp = (normed_two * gain_second).astype(jnp.bfloat16)
    expanded = jnp.dot(normed_mlp, in_full, preferred_element_type=jnp.float32)
    pre_act = expanded[:, :hidden_units]
    gate_part = expanded[:, hidden_units:]
    activated = jax.nn.gelu(pre_act, approximate=False)
    product = (activated * gate_part).astype(jnp.bfloat16)
    block_out = (
        residual
        + jnp.einsum("tf,df->td", product, mlp_turned, preferred_element_type=jnp.float32)
    ).astype(jnp.bfloat16)
    grad_out = cotangent[0]
    grad_product = jnp.einsum("td,df->tf", grad_out, mlp_turned, preferred_element_type=jnp.float32)
    grad_expanded = jnp.concatenate(
        [grad_product * gate_part * gelu_slope(pre_act), grad_product * activated], axis=1
    ).astype(jnp.bfloat16)
    grad_normed_mlp = jnp.einsum(
        "tf,df->td", grad_expanded, in_full, preferred_element_type=jnp.float32
    )
    grad_gain_two = jnp.sum(grad_normed_mlp * normed_two, axis=0)
    grad_residual = grad_out.astype(jnp.float32) + norm_back(
        grad_normed_mlp * gain_second, normed_two, scale_two
    )
    residual_half = grad_residual.astype(jnp.bfloat16)
    gain_block = jnp.pad(grad_gain_two[:, None], ((0, 0), (0, LANES - 1))).astype(jnp.bfloat16)
    weight_sums = lax.psum_scatter(
        weight_grads(
            (
                (attended, residual_half),
                (normed_mlp, grad_expanded),
                (grad_out, product),
            ),
            gain_block,
            (0, width, width + 2 * hidden_units + LANES, width + 2 * hidden_units),
            width + 3 * hidden_units + LANES,
        ),
        everyone,
        scatter_dimension=0,
        tiled=True,
    ).astype(jnp.float32)
    grad_attended = jnp.einsum(
        "te,de->td", residual_half, attn_full, preferred_element_type=jnp.float32
    ).astype(jnp.bfloat16)
    row_grad = lax.all_to_all(
        jnp.transpose(grad_attended.reshape(tok_count, ctx_size, own_width), (1, 0, 2)),
        "ctx",
        0,
        0,
        tiled=True,
    )
    row_grad_cols = row_grad.reshape(row_count, own_width).T.reshape(
        own_heads, head_size, row_count
    )
    grad_query, grad_key, grad_value = attend_grads(
        query_cols,
        key_cols,
        value_cols,
        seg_col,
        seg_row,
        log_total,
        row_grad_cols,
        row_attended,
        scale,
    )
    grad_proj_cols = (
        jnp.stack(
            [
                unrotate_cols(grad_query, cosine, sine),
                unrotate_cols(grad_key, cosine, sine),
                grad_value,
            ],
            axis=0,
        )
        .astype(jnp.bfloat16)
        .reshape(3 * own_width, row_count)
    )
    row_grad_normed = jnp.einsum(
        "de,et->td", qkv_mine, grad_proj_cols, preferred_element_type=jnp.float32
    )
    grad_gain_part = jnp.sum(row_grad_normed * row_normed, axis=0)
    grad_normed_attn = jnp.sum(
        lax.all_to_all(
            row_grad_normed.astype(jnp.bfloat16).reshape(ctx_size, tok_count, width),
            "ctx",
            0,
            0,
            tiled=True,
        ).astype(jnp.float32),
        axis=0,
    )
    qkv_terms = jnp.concatenate(
        [
            jnp.einsum(
                "td,et->de", row_normed_attn, grad_proj_cols, preferred_element_type=jnp.float32
            ).astype(jnp.bfloat16),
            jnp.pad(grad_gain_part[:, None], ((0, 0), (0, LANES - 1))).astype(jnp.bfloat16),
        ],
        axis=1,
    ).reshape(devices, weight_rows, 3 * own_width + LANES)
    qkv_sums = jnp.sum(
        lax.all_to_all(qkv_terms, everyone, 0, 0, tiled=True)
        .reshape(ctx_size, fsdp_size, weight_rows, 3 * own_width + LANES)
        .astype(jnp.float32),
        axis=1,
    )
    grad_qkv_rows = jnp.transpose(
        qkv_sums[:, :, : 3 * own_width].reshape(ctx_size, weight_rows, 3, own_width), (1, 2, 0, 3)
    ).reshape(weight_rows, 3 * width)
    gain_sum_one = jnp.sum(qkv_sums[:, :, 3 * own_width], axis=0)
    grad_tokens = (
        grad_residual + norm_back(grad_normed_attn * gain_first, normed_one, scale_one)
    ).astype(jnp.bfloat16)
    grad_attn_rows = weight_sums[:, :width]
    grad_in_rows = weight_sums[:, width : width + 2 * hidden_units]
    grad_mlp_cols = weight_sums[:, width + 2 * hidden_units + LANES :].T
    gain_sum_two = weight_sums[:, width + 2 * hidden_units]
    return (
        block_out[None],
        grad_tokens[None],
        grad_qkv_rows,
        grad_attn_rows,
        grad_in_rows,
        grad_mlp_cols,
        gain_sum_one,
        gain_sum_two,
    )


def solution(mesh):
    in_specs = (
        P("fsdp", "ctx", None),
        P("fsdp", "ctx"),
        P(("ctx", "fsdp")),
        P(("ctx", "fsdp"), None),
        P(("ctx", "fsdp"), None),
        P(("ctx", "fsdp")),
        P(("ctx", "fsdp"), None),
        P(None, ("ctx", "fsdp")),
        P("fsdp", "ctx", None),
    )
    out_specs = (
        P("fsdp", "ctx", None),
        P("fsdp", "ctx", None),
        P(("ctx", "fsdp"), None),
        P(("ctx", "fsdp"), None),
        P(("ctx", "fsdp"), None),
        P(None, ("ctx", "fsdp")),
        P(("ctx", "fsdp")),
        P(("ctx", "fsdp")),
    )
    step = functools.partial(body, mesh.shape["ctx"], mesh.shape["fsdp"])
    return jax.shard_map(step, mesh=mesh, in_specs=in_specs, out_specs=out_specs, check_vma=False)
```

profile of v0, /device:TPU:11, one launch (start us, length us, event | category | flops | bytes accessed | tf_op | source)
XLA Modules:
  0.0 486.2 jit_solution(13479057995040597754)
XLA Ops:
  7.2 2.0 pad_maximum_fusion.1
  9.8 1.1 broadcast_in_dim.17
  10.9 6.3 %all-to-all-start = ((bf16[32,32,512]{2,1,0:T(8,128)(2,1)}), bf16[32,32,512]{2,1,0:T(8,128)(2,1)S(1)}, u32[]{:S(2)}, u32[]{:S(2)}) async-start(bf16[32,32,512]{2,1,0:T(8,128)(2,1)} %bitcast.4), calls=%async_computation | async-start | bytes 2097152 | tf_op jit(solution)/shard_map/all_to_all | solution.py:249
  17.2 35.8 %all-to-all-done = bf16[32,32,512]{2,1,0:T(8,128)(2,1)S(1)} async-done(((bf16[32,32,512]{2,1,0:T(8,128)(2,1)}), bf16[32,32,512]{2,1,0:T(8,128)(2,1)S(1)}, u32[]{:S(2)}, u32[]{:S(2)}) %all-to-all-start) | async-done | bytes 1048608 | tf_op jit(solution)/shard_map/all_to_all | solution.py:249
  53.1 1.7 broadcast_in_dim.18
  54.8 5.8 %all-to-all-start.1 = ((bf16[8,144,1024]{2,1,0:T(8,128)(2,1)}), bf16[8,144,1024]{2,1,0:T(8,128)(2,1)S(1)}, u32[]{:S(2)}, u32[]{:S(2)}) async-start(bf16[8,144,1024]{2,1,0:T(8,128)(2,1)} %broadcast_in_dim.18), calls=%async_computation.1 | async-start | bytes 4718592 | tf_op jit(solution)/shard_map/all_to_all | solution.py:228
  60.7 0.5 multiply_cosine_fusion
  61.3 1.1 convert_bitcast_fusion
  62.3 0.5 slice_reduce_fusion
  62.9 96.5 %all-to-all-done.1 = bf16[8,144,1024]{2,1,0:T(8,128)(2,1)S(1)} async-done(((bf16[8,144,1024]{2,1,0:T(8,128)(2,1)}), bf16[8,144,1024]{2,1,0:T(8,128)(2,1)S(1)}, u32[]{:S(2)}, u32[]{:S(2)}) %all-to-all-start.1) | async-done | bytes 2359328 | tf_op jit(solution)/shard_map/all_to_all | solution.py:228
  159.4 0.3 convert_reduce_fusion.1
  159.7 0.7 multiply_reduce_fusion.1
  160.5 0.7 multiply_convert_fusion.1
  161.2 0.5 copy-done.11
  161.7 1.0 fusion.53
  162.7 1.1 copy-done.13
  163.9 0.7 slice.194
  164.6 1.0 copy.77.refs_3_
  165.7 1.4 fusion.79
  167.2 1.1 fusion.69
  168.3 9.9 %attend.1 = (bf16[2,64,1024]{2,1,0:T(8,128)(2,1)}, f32[2,1024,1]{2,1,0:T(8,128)}) custom-call(bf16[2,64,1024]{2,1,0:T(8,128)(2,1)} %get-tuple-element.39.refs_0_, bf16[2,64,1024]{2,1,0:T(8,128)(2,1)} %get-tuple-element.38.refs_1_, bf16[2,64,1024]{2,1,0:T(8,128)(2,1)} %bitcast.111, f32[1024,1]{1,0:T(8,128)} %copy.77.refs_3_, f32[1,1024]{1,0:T(1,128)} %bitcast.134), custom_call_target="tpu_custom_call" | custom-call | tf_op jit(solution)/shard_map/attend/pallas_call | solution.py:140
  178.2 1.1 copy.78
  179.3 13.9 %all_to_all.30 = bf16[8,128,128]{2,1,0:T(8,128)(2,1)S(1)} all-to-all(bf16[8,128,128]{2,1,0:T(8,128)(2,1)S(1)} %bitcast.123), channel_id=1, replica_groups=mesh['ctx'=8,'fsdp'=4] {'ctx'}, dimensions={0} | all-to-all | bytes 524288 | tf_op jit(solution)/shard_map/all_to_all | solution.py:281
  193.2 0.7 copy-done.16
  193.9 0.7 copy_bitcast_fusion.1.refs_0_
  194.6 2.2 fusion.82
  197.3 5.8 %fusion.2 = f32[128,5248]{1,0:T(8,128)S(1)} fusion(bf16[128,1024]{1,0:T(8,128)(2,1)S(1)} %multiply_convert_fusion.4.refs_2_, bf16[1024,8896]{1,0:T(8,128)(2,1)} %all-gather.2.cloned.1.call-done), kind=kOutput, calls=%fused_computation.2 | convolution fusion | flops 1375731712 | bytes 13697024 | tf_op jit(solution)/shard_map/dot_general | solution.py:292
  203.1 6.1 %multiply_convert_fusion.2 = (bf16[128,2624]{1,0:T(8,128)(2,1)S(1)}, f32[128,2624]{1,0:T(8,128)S(1)}, bf16[128,2624]{1,0:T(8,128)(2,1)S(1)}) fusion(f32[128,5248]{1,0:T(8,128)S(1)} %fusion.2, bf16[1024,8896]{1,0:T(8,128)(2,1)} %all-gather.2.cloned.1.call-done, bf16[1,128,1024]{2,1,0:T(8,128)(2,1)S(1)} %copy-done.14), kind=kOutput, calls=%fused_computation.36 | convolution fusion | flops 713728000 | bytes 11141120 | tf_op jit(solution)/shard_map/td,df->tf/dot_general | solution.py:302
  209.2 1.3 multiply_convert_fusion.3.refs_5_
  210.5 0.3 pad_maximum_fusion.refs_3_
  210.8 7.0 %multiply_reduce_fusion.2 = (bf16[1024]{0:T(1024)(128)(2,1)S(1)}, f32[128]{0:T(128)S(1)}, f32[128]{0:T(128)S(1)}, f32[128,1024]{1,0:T(8,128)S(1)}) fusion(f32[128,1024]{1,0:T(8,128)S(1)} %get-tuple-element.55, f32[128]{0:T(128)S(1)} %add_rsqrt_fusion.2, f32[128]{0:T(128)S(1)} %broadcast_multiply_fusion.8, f32[1024]{0:T(1024)S(1)} %get-tuple-element.23, ...), kind=kOutput, calls=%fused_computation.94 | convolution fusion | flops 1376779008 | bytes 13148160 | tf_op jit(solution)/shard_map/tf,df->td/dot_general | solution.py:306
  218.0 0.8 pad.20.refs_6_
  218.8 1.1 fusion.77
  219.9 11.6 %weight_grads.1 = bf16[1024,9024]{1,0:T(8,128)(2,1)} custom-call(bf16[128,1024]{1,0:T(8,128)(2,1)} %copy_bitcast_fusion.1.refs_0_, bf16[128,1024]{1,0:T(8,128)(2,1)} %get-tuple-element.25.refs_1_, bf16[128,1024]{1,0:T(8,128)(2,1)} %copy-done.15, bf16[128,5248]{1,0:T(8,128)(2,1)} %copy-done.1, bf16[128,1024]{1,0:T(8,128)(2,1)} %bitcast.120, ...), custom_call_target="tpu_custom_call" | custom-call | tf_op jit(solution)/shard_map/weight_grads/pallas_call | solution.py:192
  231.5 2.5 fusion.44
  234.1 0.8 copy.105
  234.8 6.1 %all-to-all-start.3 = ((bf16[8,128,128]{2,1,0:T(8,128)(2,1)}), bf16[8,128,128]{2,1,0:T(8,128)(2,1)}, u32[]{:S(2)}, u32[]{:S(2)}) async-start(bf16[8,128,128]{2,1,0:T(8,128)(2,1)} %bitcast.122), calls=%async_computation.3 | async-start | bytes 524288 | tf_op jit(solution)/shard_map/all_to_all | solution.py:333
  240.9 2.0 multiply_convert_fusion
  242.9 5.9 %all-to-all-done.3 = bf16[8,128,128]{2,1,0:T(8,128)(2,1)} async-done(((bf16[8,128,128]{2,1,0:T(8,128)(2,1)}), bf16[8,128,128]{2,1,0:T(8,128)(2,1)}, u32[]{:S(2)}, u32[]{:S(2)}) %all-to-all-start.3) | async-done | bytes 262176 | tf_op jit(solution)/shard_map/all_to_all | solution.py:333
  248.9 1.8 copy.82
  250.6 9.5 %attend_grads.1 = (f32[2,64,1024]{2,1,0:T(8,128)}, f32[2,64,1024]{2,1,0:T(8,128)}, f32[2,64,1024]{2,1,0:T(8,128)}) custom-call(bf16[2,64,1024]{2,1,0:T(8,128)(2,1)} %get-tuple-element.39.refs_0_, bf16[2,64,1024]{2,1,0:T(8,128)(2,1)} %get-tuple-element.38.refs_1_, bf16[2,64,1024]{2,1,0:T(8,128)(2,1)} %bitcast.112, f32[1024,1]{1,0:T(8,128)} %copy.77.refs_3_, ...), custom_call_target="tpu_custom_call" | custom-call | tf_op jit(solution)/shard_map/attend_grads/pallas_call | solution.py:160
  260.2 1.3 broadcast_multiply_fusion.1
  261.6 0.8 copy-done.5
  263.0 0.8 copy-done.17
  263.9 0.3 copy-done.12
  264.3 2.9 multiply_reduce_fusion
  267.2 1.0 convolution_convert_fusion
  268.3 0.5 copy.84
  268.8 44.8 %all_to_all.31 = bf16[32,32,512]{2,1,0:T(8,128)(2,1)} all-to-all(bf16[32,32,512]{2,1,0:T(8,128)(2,1)S(1)} %bitcast.110), channel_id=1, replica_groups=mesh['ctx'=8,'fsdp'=4] {'ctx','fsdp'}, dimensions={0} | all-to-all | bytes 2097152 | tf_op jit(solution)/shard_map/all_to_all | solution.py:390
  313.7 7.9 %all-to-all-start.4 = ((bf16[8,128,1024]{2,1,0:T(8,128)(2,1)}), bf16[8,128,1024]{2,1,0:T(8,128)(2,1)S(1)}, u32[]{:S(2)}, u32[]{:S(2)}) async-start(bf16[8,128,1024]{2,1,0:T(8,128)(2,1)} %bitcast.115), calls=%async_computation.4 | async-start | bytes 4194304 | tf_op jit(solution)/shard_map/all_to_all | solution.py:371
  321.9 5.6 %fusion.47 = bf16[1,128,1024]{2,1,0:T(8,128)(2,1)} fusion(f32[128,1024]{1,0:T(8,128)S(1)} %get-tuple-element.55, bf16[128,2624]{1,0:T(8,128)(2,1)} %multiply_convert_fusion.3.refs_5_, bf16[1024,8896]{1,0:T(8,128)(2,1)} %all-gather.2.cloned.1.call-done), kind=kOutput, calls=%fused_computation.59 | convolution fusion | flops 688128000 | bytes 6979584 | tf_op jit(solution)/shard_map/tf,df->td/dot_general | solution.py:299
  327.7 1.0 reshape.223
  328.7 1.3 copy.85
  330.0 0.8 copy.104
  330.8 0.6 slice_reduce_fusion.2
  331.4 36.0 %all-to-all-done.4 = bf16[8,128,1024]{2,1,0:T(8,128)(2,1)S(1)} async-done(((bf16[8,128,1024]{2,1,0:T(8,128)(2,1)}), bf16[8,128,1024]{2,1,0:T(8,128)(2,1)S(1)}, u32[]{:S(2)}, u32[]{:S(2)}) %all-to-all-start.4) | async-done | bytes 2097184 | tf_op jit(solution)/shard_map/all_to_all | solution.py:371
  367.4 0.3 convert_reduce_fusion
  368.0 1.0 fusion.73
  369.0 106.2 %reduce-scatter.2.cloned.1.call-done = bf16[32,9024]{1,0:T(8,128)(2,1)} async-done(((bf16[1024,9024]{1,0:T(8,128)(2,1)}), bf16[32,9024]{1,0:T(8,128)(2,1)}) %reduce-scatter.2.cloned.1.call-update) | async-done | bytes 577552 | tf_op jit(solution)/shard_map/reduce_scatter | solution.py:315
  475.2 1.2 convert_element_type.150
  476.4 0.8 slice_bitcast_fusion
  477.1 0.6 slice_reduce_fusion.3
  477.8 0.7 slice.139
  478.4 0.9 slice.140
  (85 shorter events, 3.1 us)
Async XLA Ops:
  7.2 2.1 copy-start.20
  7.2 2.1 copy-start.21
  7.2 2.2 copy-start.18
  7.2 187.4 %all-gather.2.cloned.1.call-start = ((), (), s32[]{:S(2)}) async-start(), calls=%async_computation.7 | async-start | bytes 18923520 | tf_op jit(solution)/shard_map/all_gather | solution.py:258
  10.9 6.3 %copy-start.22 = (s32[1,128]{1,0:T(1,128)S(1)}, s32[1,128]{1,0:T(1,128)}, u32[]{:S(2)}) copy-start(s32[1,128]{1,0:T(1,128)} %param.10) | copy-start | bytes 1540
  10.9 6.3 %copy-start = (bf16[1,128,1024]{2,1,0:T(8,128)(2,1)S(1)}, bf16[1,128,1024]{2,1,0:T(8,128)(2,1)}, u32[]{:S(2)}) copy-start(bf16[1,128,1024]{2,1,0:T(8,128)(2,1)} %param.9) | copy-start | bytes 786436
  10.9 42.2 %all-to-all-start = ((bf16[32,32,512]{2,1,0:T(8,128)(2,1)}), bf16[32,32,512]{2,1,0:T(8,128)(2,1)S(1)}, u32[]{:S(2)}, u32[]{:S(2)}) async-start(bf16[32,32,512]{2,1,0:T(8,128)(2,1)} %bitcast.4), calls=%async_computation | async-start | bytes 2097152 | tf_op jit(solution)/shard_map/all_to_all | solution.py:249
  53.1 1.8 copy-start.10
  54.8 104.6 %all-to-all-start.1 = ((bf16[8,144,1024]{2,1,0:T(8,128)(2,1)}), bf16[8,144,1024]{2,1,0:T(8,128)(2,1)S(1)}, u32[]{:S(2)}, u32[]{:S(2)}) async-start(bf16[8,144,1024]{2,1,0:T(8,128)(2,1)} %broadcast_in_dim.18), calls=%async_computation.1 | async-start | bytes 4718592 | tf_op jit(solution)/shard_map/all_to_all | solution.py:228
  60.6 414.5 %reduce-scatter.2.cloned.1.call-start = ((), (), s32[]{:S(2)}) async-start(), calls=%async_computation.8 | async-start | bytes 19193856 | tf_op jit(solution)/shard_map/reduce_scatter | solution.py:315
  61.3 106.0 %copy-start.4 = (f32[64,1024]{1,0:T(8,128)}, f32[64,1024]{1,0:T(8,128)S(1)}, u32[]{:S(2)}) copy-start(f32[64,1024]{1,0:T(8,128)S(1)} %get-tuple-element.58) | copy-start | bytes 786436
  160.5 1.2 copy-start.11
  162.7 1.2 copy-start.13
  164.6 2.6 copy-start.19
  193.2 0.7 copy-start.16
  197.2 5.8 %copy-start.15 = (bf16[128,1024]{1,0:T(8,128)(2,1)}, bf16[128,1024]{1,0:T(8,128)(2,1)S(1)}, u32[]{:S(2)}) copy-start(bf16[128,1024]{1,0:T(8,128)(2,1)S(1)} %multiply_convert_fusion.4.refs_2_) | copy-start | bytes 786436
  197.3 5.8 %copy-start.14 = (bf16[1,128,1024]{2,1,0:T(8,128)(2,1)S(1)}, bf16[1,128,1024]{2,1,0:T(8,128)(2,1)}, u32[]{:S(2)}) copy-start(bf16[1,128,1024]{2,1,0:T(8,128)(2,1)} %param.17) | copy-start | bytes 786436
  210.8 7.0 %copy-start.1 = (bf16[128,5248]{1,0:T(8,128)(2,1)}, bf16[128,5248]{1,0:T(8,128)(2,1)S(1)}, u32[]{:S(2)}) copy-start(bf16[128,5248]{1,0:T(8,128)(2,1)S(1)} %pad_maximum_fusion.refs_3_) | copy-start | bytes 4030468
  234.8 14.0 %all-to-all-start.3 = ((bf16[8,128,128]{2,1,0:T(8,128)(2,1)}), bf16[8,128,128]{2,1,0:T(8,128)(2,1)}, u32[]{:S(2)}, u32[]{:S(2)}) async-start(bf16[8,128,128]{2,1,0:T(8,128)(2,1)} %bitcast.122), calls=%async_computation.3 | async-start | bytes 524288 | tf_op jit(solution)/shard_map/all_to_all | solution.py:333
  261.5 1.0 copy-start.5
  261.5 1.1 copy-start.8
  261.5 1.3 copy-start.9
  262.8 1.1 copy-start.17
  263.0 1.3 copy-start.12
  264.3 2.9 copy-start.6
  313.7 53.7 %all-to-all-start.4 = ((bf16[8,128,1024]{2,1,0:T(8,128)(2,1)}), bf16[8,128,1024]{2,1,0:T(8,128)(2,1)S(1)}, u32[]{:S(2)}, u32[]{:S(2)}) async-start(bf16[8,128,1024]{2,1,0:T(8,128)(2,1)} %bitcast.115), calls=%async_computation.4 | async-start | bytes 4194304 | tf_op jit(solution)/shard_map/all_to_all | solution.py:371
  321.9 5.6 %copy-start.2 = (bf16[32,32,512]{2,1,0:T(8,128)(2,1)S(1)}, bf16[32,32,512]{2,1,0:T(8,128)(2,1)}, u32[]{:S(2)}) copy-start(bf16[32,32,512]{2,1,0:T(8,128)(2,1)} %all_to_all.31) | copy-start | bytes 3145732
  331.4 36.6 %copy-start.7 = (f32[128,1024]{1,0:T(8,128)S(1)}, f32[128,1024]{1,0:T(8,128)}, u32[]{:S(2)}) copy-start(f32[128,1024]{1,0:T(8,128)} %get-tuple-element.26) | copy-start | bytes 1572868
  475.2 2.6 copy-start.3
Sparse Core Ops, SparseCore 0:
  11.5 169.8 all-gather.1
  231.7 243.4 reduce-scatter.1
where the time goes:
time: 488 us; the launch traced here: 486 us
  waiting for transfers between devices  281 us (58%)
  blocking collectives  58.7 us (12%)
  matrix products  34 us (7%)
  Pallas kernels  31 us (6%)
  starting transfers between devices  26.1 us (5%)
  local copies, waits for them, and re-layouts  23.7 us (5%)
  other arithmetic  17.5 us (4%)
  between operations  14.6 us (3%)
    reduce_scatter x1, waiting for transfers between devices, body(): lax.psum_scatter(weight_grads(((attended, residual_half), (normed_mlp, gr...  106 us
    all_to_all x1, waiting for transfers between devices, body(): lax.all_to_all(jnp.broadcast_to(jnp.concatenate([inputs[0], seg_block], a...  96.5 us
    all_to_all x1, blocking collectives, body(): lax.all_to_all(qkv_terms, everyone, 0, 0, tiled=True)  44.8 us
    all_to_all x1, waiting for transfers between devices, body(): lax.all_to_all(row_grad_normed.astype(jnp.bfloat16).reshape(ctx_size, tok...  36 us
    all_to_all x1, waiting for transfers between devices, body(): lax.all_to_all(qkv_parts, everyone, 0, 0, tiled=True)  35.8 us
    all_to_all x1, blocking collectives, body(): lax.all_to_all(row_attended.reshape(own_width, row_count).T.reshape(ctx_s...  13.9 us
    pallas_call x1, Pallas kernels, weight_grads(): pl.pallas_call(lambda *refs: weight_grads_kernel(bounds, *refs), grid=(wi...  11.6 us
    pallas_call x1, Pallas kernels, attend(): pl.pallas_call(lambda *refs: attend_kernel(scale, *refs), grid=(heads, ro...  9.86 us
  transfers between devices with their start and end apart: 6, of which 5 were waited for; matrix products, arithmetic and copies ran while one was open for 8% of the time, Pallas kernels for 4%

commit v1 on v0

v1 whole, which is shorter than its diff:
```python
import functools
import math

import jax
import jax.numpy as jnp
from jax import lax
from jax.experimental import pallas as pl
from jax.experimental.pallas import tpu as pltpu
from jax.sharding import PartitionSpec as P

HEADS = 16
HD = 64


EPSILON = 1e-05
ROPE_BASE = 160000.0
MASKED = -1e30


def layer_norm(values):
    center = values - jnp.mean(values, axis=-1, keepdims=True)
    scaled = lax.rsqrt(jnp.mean(center * center, axis=-1, keepdims=True) + EPSILON)
    return (center * scaled, scaled)


def norm_back(grad_norm, normed, scaled):
    return scaled * (
        grad_norm
        - jnp.mean(grad_norm, axis=-1, keepdims=True)
        - normed * jnp.mean(grad_norm * normed, axis=-1, keepdims=True)
    )


def rope_columns(positions, head_size):
    freqs = ROPE_BASE ** (-jnp.arange(0, head_size, 2, dtype=jnp.float32) / head_size)
    angles = freqs[:, None] * positions[None, :]
    cosine = jnp.concatenate([jnp.cos(angles), jnp.cos(angles)], axis=0)
    sine = jnp.concatenate([jnp.sin(angles), jnp.sin(angles)], axis=0)
    return (cosine[None], sine[None])


def rotate_cols(values, cosine, sine):
    half = values.shape[1] // 2
    turned = jnp.concatenate([-values[:, half:], values[:, :half]], axis=1)
    return values * cosine + turned * sine


def unrotate_cols(grads, cosine, sine):
    half = grads.shape[1] // 2
    weighted = grads * sine
    turned = jnp.concatenate([weighted[:, half:], -weighted[:, :half]], axis=1)
    return grads * cosine + turned


def gelu_slope(values):
    return (
        0.5 * (1.0 + lax.erf(values * 0.7071067811865476))
        + values * jnp.exp(-0.5 * values * values) * 0.3989422804014327
    )


LANES = 128
QUERY_BLOCK = 256


def masked_scores(query, key, same, scale):
    scores = lax.dot_general(query, key, (((0,), (0,)), ((), ())), preferred_element_type=jnp.float32)
    return jnp.where(same, scores * scale, MASKED)


def attend_kernel(scale, query_ref, key_ref, value_ref, seg_own_ref, seg_ref, out_ref, log_ref):
    same = seg_own_ref[...] == seg_ref[...]
    scores = masked_scores(query_ref[0], key_ref[0], same, scale)
    peak = jnp.max(scores, axis=-1, keepdims=True)
    log_total = peak + jnp.log(jnp.sum(jnp.exp(scores - peak), axis=-1, keepdims=True))
    log_ref[0] = log_total
    probs = jnp.exp(scores - log_total).astype(jnp.bfloat16)
    out_ref[0] = lax.dot_general(
        value_ref[0], probs, (((1,), (1,)), ((), ())), preferred_element_type=jnp.float32
    ).astype(jnp.bfloat16)


def attend_grad_kernel(
    scale,
    query_ref,
    key_ref,
    value_ref,
    seg_own_ref,
    seg_ref,
    log_ref,
    grad_ref,
    attended_ref,
    query_grad_ref,
    key_grad_ref,
    value_grad_ref,
):
    @pl.when(pl.program_id(1) == 0)
    def _():
        key_grad_ref[...] = jnp.zeros_like(key_grad_ref)
        value_grad_ref[...] = jnp.zeros_like(value_grad_ref)

    query = query_ref[0]
    grad = grad_ref[0]
    key = key_ref[0]
    dots_row = jnp.sum(
        grad.astype(jnp.float32) * attended_ref[0].astype(jnp.float32), axis=0, keepdims=True
    )
    dots = jnp.transpose(jnp.broadcast_to(dots_row, (8, dots_row.shape[1])))[:, :1]
    same = seg_own_ref[...] == seg_ref[...]
    probs = jnp.exp(masked_scores(query, key, same, scale) - log_ref[0])
    grad_probs = lax.dot_general(
        grad, value_ref[0], (((0,), (0,)), ((), ())), preferred_element_type=jnp.float32
    )
    grad_scores = (probs * (grad_probs - dots)).astype(jnp.bfloat16)
    query_grad_ref[0] = scale * lax.dot_general(
        key, grad_scores, (((1,), (1,)), ((), ())), preferred_element_type=jnp.float32
    )
    key_grad_ref[0] += scale * lax.dot_general(
        query, grad_scores, (((1,), (0,)), ((), ())), preferred_element_type=jnp.float32
    )
    value_grad_ref[0] += lax.dot_general(
        grad, probs.astype(jnp.bfloat16), (((1,), (0,)), ((), ())), preferred_element_type=jnp.float32
    )


def attention_specs(head_size, row_count, block):
    part = pl.BlockSpec((1, head_size, block), lambda h, b: (h, 0, b))
    full = pl.BlockSpec((1, head_size, row_count), lambda h, b: (h, 0, 0))
    seg_own = pl.BlockSpec((block, 1), lambda h, b: (b, 0))
    seg_all = pl.BlockSpec((1, row_count), lambda h, b: (0, 0))
    log = pl.BlockSpec((1, block, 1), lambda h, b: (h, b, 0))
    return part, full, seg_own, seg_all, log


def attend(query_cols, key_cols, value_cols, seg_col, seg_row, scale):
    heads, head_size, row_count = query_cols.shape
    block = min(QUERY_BLOCK, row_count)
    part, full, own, every, log = attention_specs(head_size, row_count, block)
    return pl.pallas_call(
        lambda *refs: attend_kernel(scale, *refs),
        grid=(heads, row_count // block),
        in_specs=[part, full, full, own, every],
        out_specs=[part, log],
        out_shape=[
            jax.ShapeDtypeStruct((heads, head_size, row_count), jnp.bfloat16),
            jax.ShapeDtypeStruct((heads, row_count, 1), jnp.float32),
        ],
        name="attend",
    )(query_cols, key_cols, value_cols, seg_col, seg_row)


def attend_grads(
    query_cols, key_cols, value_cols, seg_col, seg_row, log_total, grad_cols, attended_cols, scale
):
    heads, head_size, row_count = query_cols.shape
    block = min(QUERY_BLOCK, row_count)
    part, full, own, every, log = attention_specs(head_size, row_count, block)
    grads = jax.ShapeDtypeStruct((heads, head_size, row_count), jnp.float32)
    return pl.pallas_call(
        lambda *refs: attend_grad_kernel(scale, *refs),
        grid=(heads, row_count // block),
        in_specs=[part, full, full, own, every, log, part, part],
        out_specs=[part, full, full],
        out_shape=[grads, grads, grads],
        name="attend_grads",
    )(query_cols, key_cols, value_cols, seg_col, seg_row, log_total, grad_cols, attended_cols)


MESH = pl.DeviceIdType.MESH


class Links:
    def __init__(self, ctx_size, fsdp_size, send_sems, recv_sems, local_sems):
        self.ctx_size = ctx_size
        self.fsdp_size = fsdp_size
        self.ctx = lax.axis_index("ctx")
        self.fsdp = lax.axis_index("fsdp")
        self.send_sems = send_sems
        self.recv_sems = recv_sems
        self.local_sems = local_sems
        self.used = 0
        self.used_local = 0

    def slot(self):
        self.used += 1
        return self.used - 1

    def ctx_copy(self, slot, src, dst, peer):
        return pltpu.make_async_remote_copy(
            src_ref=src,
            dst_ref=dst,
            send_sem=self.send_sems.at[slot],
            recv_sem=self.recv_sems.at[slot],
            device_id={"ctx": peer},
            device_id_type=MESH,
        )

    def fsdp_copy(self, slot, src, dst, peer):
        return pltpu.make_async_remote_copy(
            src_ref=src,
            dst_ref=dst,
            send_sem=self.send_sems.at[slot],
            recv_sem=self.recv_sems.at[slot],
            device_id={"fsdp": peer},
            device_id_type=MESH,
        )

    def local(self, src, dst):
        self.used_local += 1
        return pltpu.make_async_copy(src, dst, self.local_sems.at[self.used_local - 1])

    def barrier(self, over_ctx, over_fsdp):
        sem = pltpu.get_barrier_semaphore()
        count = 0
        if over_ctx:
            for k in range(1, self.ctx_size):
                pl.semaphore_signal(sem, inc=1, device_id={"ctx": self.ctx ^ k}, device_id_type=MESH)
                count += 1
        if over_fsdp:
            for k in range(1, self.fsdp_size):
                pl.semaphore_signal(sem, inc=1, device_id={"fsdp": self.fsdp ^ k}, device_id_type=MESH)
                count += 1
        pl.semaphore_wait(sem, count)


def run_tasks(tasks):
    live = list(tasks)
    while live:
        left = []
        for task in live:
            try:
                next(task)
                left.append(task)
            except StopIteration:
                pass
        live = left


def gather_ctx(links, own, place):
    c, n = links.ctx, links.ctx_size
    line = n // 2
    pos = c // 2
    pair_slots = {}
    right_slots = [None] + [links.slot() for s in range(1, line)]
    left_slots = [None] + [links.slot() for s in range(1, line)]
    own_slot = links.slot()
    from_left_slots = [None] + [links.slot() for s in range(1, line)]
    from_right_slots = [None] + [links.slot() for s in range(1, line)]

    def block(step):
        return (c + 2 * step + n) % n

    def right(step):
        source = own if step == 1 else place(block(1 - step))
        return links.ctx_copy(right_slots[step], source, place(block(1 - step)), (c + 2) % n)

    def left(step):
        source = own if step == 1 else place(block(step - 1))
        return links.ctx_copy(left_slots[step], source, place(block(step - 1)), (c + n - 2) % n)

    def pair(step):
        if step == 0:
            return links.ctx_copy(own_slot, own, place(c), c ^ 1)
        slot = from_left_slots[-step] if step < 0 else from_right_slots[step]
        return links.ctx_copy(slot, place(block(step)), place(block(step)), c ^ 1)

    def arrived_from_left(step):
        return links.ctx_copy(right_slots[step], own, place(block(-step)), c ^ 1)

    def arrived_from_right(step):
        return links.ctx_copy(left_slots[step], own, place(block(step)), c ^ 1)

    if line > 1:
        @pl.when(pos < line - 1)
        def _():
            right(1).start()

        @pl.when(pos > 0)
        def _():
            left(1).start()

    pair(0).start()
    yield
    for step in range(1, line):
        @pl.when(pos >= step)
        def _():
            arrived_from_left(step).wait_recv()
            if step < line - 1:
                @pl.when(pos < line - 1)
                def _():
                    right(step + 1).start()
            pair(-step).start()

        @pl.when(pos + step < line)
        def _():
            arrived_from_right(step).wait_recv()
            if step < line - 1:
                @pl.when(pos > 0)
                def _():
                    left(step + 1).start()
            pair(step).start()

        yield
    pair(0).wait_send()
    links.ctx_copy(own_slot, own, place(c ^ 1), c ^ 1).wait_recv()
    for step in range(1, line):
        @pl.when(pos < line - 1)
        def _():
            @pl.when(pos >= step - 1)
            def _():
                right(step).wait_send()

        @pl.when(pos > 0)
        def _():
            @pl.when(pos + step - 1 < line)
            def _():
                left(step).wait_send()

        @pl.when(pos >= step)
        def _():
            pair(-step).wait_send()
            links.ctx_copy(from_left_slots[step], own, place(block(-step) ^ 1), c ^ 1).wait_recv()

        @pl.when(pos + step < line)
        def _():
            pair(step).wait_send()
            links.ctx_copy(from_right_slots[step], own, place(block(step) ^ 1), c ^ 1).wait_recv()


def spread_ctx(links, source, place, arrived):
    copies = []
    for k in reversed(range(1, links.ctx_size)):
        peer = links.ctx ^ k
        slot = links.slot()
        links.ctx_copy(slot, source(peer), place(), peer).start()
        copies.append((slot, peer))
    yield
    for slot, peer in copies:
        links.ctx_copy(slot, source(peer), arrived(peer), peer).wait()


def spread_fsdp(links, source, place, arrived):
    copies = []
    for k in reversed(range(1, links.fsdp_size)):
        peer = links.fsdp ^ k
        slot = links.slot()
        links.fsdp_copy(slot, source(peer), place(), peer).start()
        copies.append((slot, peer))
    yield
    for slot, peer in copies:
        links.fsdp_copy(slot, source(peer), arrived(peer), peer).wait()


def gather_fsdp(links, own, place):
    f = links.fsdp
    far = []
    for k in range(2, links.fsdp_size, 2):
        slot = links.slot()
        links.fsdp_copy(slot, own, place(f), f ^ k).start()
        far.append((k, slot))
    near = links.slot()
    links.fsdp_copy(near, own, place(f), f ^ 1).start()
    yield
    passed = []
    for k, slot in far:
        links.fsdp_copy(slot, own, place(f ^ k), f ^ k).wait_recv()
        onward = links.slot()
        links.fsdp_copy(onward, place(f ^ k), place(f ^ k), f ^ 1).start()
        passed.append((k, onward))
    yield
    links.fsdp_copy(near, own, place(f ^ 1), f ^ 1).wait()
    for k, slot in far:
        links.fsdp_copy(slot, own, place(f), f ^ k).wait_send()
    for k, onward in passed:
        links.fsdp_copy(onward, place(f ^ k), place(f ^ 1 ^ k), f ^ 1).wait()


def local_task(links, pairs):
    copies = [links.local(src, dst) for src, dst in pairs]
    for copy in copies:
        copy.start()
    yield
    yield
    yield
    for copy in copies:
        copy.wait()


def after(first, second):
    yield from first
    yield from second()


def exchange(name, number, sizes, make_tasks, operands, outs, over_ctx=True, over_fsdp=True, slots=96):
    ctx_size, fsdp_size = sizes

    def kernel(*refs):
        ins = refs[: len(operands)]
        results = refs[len(operands) : len(operands) + len(outs)]
        send_sems, recv_sems, local_sems = refs[len(operands) + len(outs) :]
        links = Links(ctx_size, fsdp_size, send_sems, recv_sems, local_sems)
        links.barrier(over_ctx, over_fsdp)
        run_tasks(make_tasks(links, ins, results))

    anywhere = pl.BlockSpec(memory_space=pl.ANY)
    return pl.pallas_call(
        kernel,
        in_specs=[anywhere] * len(operands),
        out_specs=[anywhere] * len(outs),
        out_shape=[jax.ShapeDtypeStruct(shape, dtype) for shape, dtype in outs],
        scratch_shapes=[
            pltpu.SemaphoreType.DMA((slots,)),
            pltpu.SemaphoreType.DMA((slots,)),
            pltpu.SemaphoreType.DMA((16,)),
        ],
        compiler_params=pltpu.CompilerParams(collective_id=number, has_side_effects=True),
        name=name,
    )(*operands)


def gather_all(sizes, tokens, seg, qkv_parts, out_rows, in_parts, mlp_parts, grad_out):
    n, fs = sizes
    bf16 = jnp.bfloat16

    def tasks(links, ins, outs):
        tokens_ref, seg_ref, qkv_ref, out_ref, in_ref, mlp_ref, grad_ref = ins
        tokens_all, seg_all, qkv_all, out_all, in_all, mlp_all, grad_all = outs
        c, f = links.ctx, links.fsdp
        chip, core = f // 2, f % 2
        staged = [
            (qkv_ref.at[c], qkv_all.at[c, f]),
            (out_ref, out_all.at[c, chip, core]),
            (in_ref.at[f], in_all.at[c, f]),
            (mlp_ref.at[f], mlp_all.at[c, f]),
        ]
        copies = [links.local(src, dst) for src, dst in staged]
        for copy in copies:
            copy.start()

        def weights(source_ref, all_ref, copy):
            def spread():
                yield from spread_fsdp(
                    links,
                    lambda peer: source_ref.at[peer],
                    lambda: all_ref.at[c, f],
                    lambda peer: all_ref.at[c, peer],
                )
                copy.wait()
                yield from gather_ctx(links, all_ref.at[c], lambda b: all_ref.at[b])
            return spread()

        def qkv():
            yield from spread_ctx(
                links,
                lambda peer: qkv_ref.at[peer],
                lambda: qkv_all.at[c, f],
                lambda peer: qkv_all.at[peer, f],
            )
            copies[0].wait()
            yield from gather_fsdp(links, qkv_all.at[:, f], lambda b: qkv_all.at[:, b])

        def out_weights():
            far = []
            for k in range(2, fs, 2):
                slot = links.slot()
                links.fsdp_copy(slot, out_ref, out_all.at[c, chip, core], f ^ k).start()
                far.append((slot, k))
            yield
            for slot, k in far:
                links.fsdp_copy(slot, out_ref, out_all.at[c, (f ^ k) // 2, core], f ^ k).wait()
            copies[1].wait()
            yield from gather_ctx(links, out_all.at[c, :, core], lambda b: out_all.at[b, :, core])
            slot = links.slot()
            links.fsdp_copy(slot, out_all.at[:, :, core], out_all.at[:, :, core], f ^ 1).start()
            yield
            links.fsdp_copy(slot, out_all.at[:, :, core], out_all.at[:, :, 1 - core], f ^ 1).wait()

        return [
            qkv(),
            gather_ctx(links, tokens_ref, lambda b: tokens_all.at[b]),
            spread_ctx(links, lambda peer: seg_ref, lambda: seg_all.at[c], lambda peer: seg_all.at[peer]),
            out_weights(),
            weights(in_ref, in_all, copies[2]),
            weights(mlp_ref, mlp_all, copies[3]),
            gather_fsdp(links, grad_ref, lambda b: grad_all.at[b]),
            local_task(
                links,
                [(tokens_ref, tokens_all.at[c]), (seg_ref, seg_all.at[c]), (grad_ref, grad_all.at[f])],
            ),
        ]

    outs = [
        ((n,) + tokens.shape, bf16),
        ((n,) + seg.shape, seg.dtype),
        ((n, fs) + qkv_parts.shape[1:], bf16),
        ((n, fs // 2, 2) + out_rows.shape, bf16),
        ((n, fs) + in_parts.shape[1:], bf16),
        ((n, fs) + mlp_parts.shape[1:], bf16),
        ((fs,) + grad_out.shape, bf16),
    ]
    return exchange(
        "gather_all",
        1,
        sizes,
        tasks,
        (tokens, seg, qkv_parts, out_rows, in_parts, mlp_parts, grad_out),
        outs,
        slots=12 * (n + fs),
    )


def swap_task(links, axis, src, out):
    me = links.ctx if axis == "ctx" else links.fsdp
    spread = spread_ctx if axis == "ctx" else spread_fsdp
    yield from spread(links, lambda peer: src.at[peer], lambda: out.at[me], lambda peer: out.at[peer])


def swaps(name, number, sizes, axes, arrays):
    def tasks(links, ins, outs):
        result = []
        own = []
        for axis, src, out in zip(axes, ins, outs):
            me = links.ctx if axis == "ctx" else links.fsdp
            if axis == "gather":
                result.append(gather_fsdp(links, src, lambda b, out=out: out.at[b]))
                own.append((src, out.at[me]))
            else:
                result.append(swap_task(links, axis, src, out))
                own.append((src.at[me], out.at[me]))
        return result + [local_task(links, own)]

    outs = [
        (((sizes[1],) if axis == "gather" else ()) + array.shape, array.dtype)
        for axis, array in zip(axes, arrays)
    ]
    return exchange(
        name,
        number,
        sizes,
        tasks,
        tuple(arrays),
        outs,
        over_ctx="ctx" in axes,
        over_fsdp="fsdp" in axes or "gather" in axes,
        slots=4 * (sizes[0] + sizes[1]),
    )


def pair_stage(number, sizes, halves, fsdp_arrays):
    n, fs = sizes

    def tasks(links, ins, outs):
        c = links.ctx
        result = []
        for src, out in zip(ins[: len(halves)], outs):
            def send(src=src, out=out):
                slots = []
                for q in range(n // 2):
                    slot = links.slot()
                    slots.append(slot)
                    links.ctx_copy(slot, src.at[q, 1 - c % 2], out.at[q], c ^ 1).start()
                yield
                for q, slot in enumerate(slots):
                    links.ctx_copy(slot, src.at[q, 1 - c % 2], out.at[q], c ^ 1).wait()
            result.append(send())
        own = []
        for src, out in zip(ins[len(halves) :], outs[len(halves) :]):
            result.append(swap_task(links, "fsdp", src, out))
            own.append((src.at[links.fsdp], out.at[links.fsdp]))
        return result + [local_task(links, own)]

    outs = [((array.shape[0],) + array.shape[2:], array.dtype) for array in halves]
    outs += [(array.shape, array.dtype) for array in fsdp_arrays]
    return exchange("pair_stage", number, sizes, tasks, tuple(halves) + tuple(fsdp_arrays), outs)


def line_stage(number, sizes, lines, ctx_arrays):
    n, fs = sizes

    def tasks(links, ins, outs):
        c = links.ctx
        pos = c // 2
        result = []
        own = []
        for src, out in zip(ins[: len(lines)], outs):
            own.append((src.at[pos], out.at[pos]))
            def send(src=src, out=out):
                slots = []
                for k in reversed(range(1, n // 2)):
                    slot = links.slot()
                    slots.append((slot, k))
                    links.ctx_copy(slot, src.at[pos ^ k], out.at[pos], c ^ (2 * k)).start()
                yield
                for slot, k in slots:
                    links.ctx_copy(slot, src.at[pos ^ k], out.at[pos ^ k], c ^ (2 * k)).wait()
            result.append(send())
        for src, out in zip(ins[len(lines) :], outs[len(lines) :]):
            result.append(swap_task(links, "ctx", src, out))
            own.append((src.at[c], out.at[c]))
        return result + [local_task(links, own)]

    outs = [(array.shape, array.dtype) for array in tuple(lines) + tuple(ctx_arrays)]
    return exchange(
        "line_stage", number, sizes, tasks, tuple(lines) + tuple(ctx_arrays), outs, over_fsdp=False
    )


def pick(array, index, axis):
    return lax.dynamic_index_in_dim(array, index, axis, keepdims=False)


def body(
    ctx_size,
    fsdp_size,
    inputs,
    segment_ids,
    gain_attn,
    w_qkv,
    w_out_attn,
    gain_mlp,
    w_in,
    w_out_mlp,
    cotangent,
):
    tok_count, width = inputs.shape[1:]
    heads = HEADS
    head_size = HD
    scale = 1.0 / math.sqrt(head_size)
    hidden_units = w_out_mlp.shape[0]
    row_count = ctx_size * tok_count
    own_heads = heads // ctx_size
    own_width = own_heads * head_size
    weight_rows = w_qkv.shape[0]
    own_hidden = hidden_units // fsdp_size
    own_out = width // fsdp_size
    line = ctx_size // 2
    block_rows = width // ctx_size
    sizes = (ctx_size, fsdp_size)
    bf16 = jnp.bfloat16
    f32 = jnp.float32
    ctx_index = lax.axis_index("ctx")
    parity = ctx_index % 2
    pos = ctx_index // 2

    qkv_parts = jnp.transpose(
        w_qkv.reshape(weight_rows, 3, ctx_size, own_width), (2, 0, 1, 3)
    ).reshape(ctx_size, weight_rows, 3 * own_width)
    gains_own = jnp.pad(jnp.stack([gain_attn, gain_mlp], axis=1), ((0, 0), (0, LANES - 2)))
    qkv_parts = jnp.concatenate(
        [qkv_parts, jnp.broadcast_to(gains_own, (ctx_size, weight_rows, LANES))], axis=2
    )
    in_parts = jnp.transpose(
        w_in.reshape(weight_rows, 2, fsdp_size, own_hidden), (2, 0, 1, 3)
    ).reshape(fsdp_size, weight_rows, 2 * own_hidden)
    mlp_parts = jnp.transpose(w_out_mlp.reshape(fsdp_size, own_hidden, weight_rows), (0, 2, 1))
    seg_own = jnp.broadcast_to(segment_ids.astype(f32), (8, tok_count))

    tokens_all, seg_all, qkv_all, out_all, in_all, mlp_all, grad_out_group = gather_all(
        sizes, inputs[0], seg_own, qkv_parts, w_out_attn, in_parts, mlp_parts, cotangent[0]
    )
    qkv_got = qkv_all.reshape(width, 3 * own_width + LANES)
    qkv_mine = qkv_got[:, : 3 * own_width]
    gains = qkv_got[:, 3 * own_width : 3 * own_width + 2].astype(f32).T
    gain_first = gains[0]
    gain_second = gains[1]
    attn_full = out_all.reshape(width, width)
    in_mine = in_all.reshape(width, 2 * own_hidden)
    mlp_turned = mlp_all.reshape(width, own_hidden)

    seg_row = seg_all[:, 0].reshape(1, row_count)
    seg_col = seg_row.reshape(row_count, 1)
    row_tokens = tokens_all.reshape(row_count, width).astype(f32)
    row_normed, unused = layer_norm(row_tokens)
    row_normed_attn = (row_normed * gain_first).astype(bf16)
    tokens = inputs[0].astype(f32)
    normed_one, scale_one = layer_norm(tokens)

    projected_cols = jnp.einsum(
        "de,td->et", qkv_mine, row_normed_attn, preferred_element_type=f32
    ).reshape(3, own_heads, head_size, row_count)
    positions = jnp.arange(row_count, dtype=jnp.int32).astype(f32)
    cosine, sine = rope_columns(positions, head_size)
    query_cols = rotate_cols(projected_cols[0], cosine, sine).astype(bf16)
    key_cols = rotate_cols(projected_cols[1], cosine, sine).astype(bf16)
    value_cols = projected_cols[2].astype(bf16)
    row_attended, log_total = attend(query_cols, key_cols, value_cols, seg_col, seg_row, scale)

    (attended,) = swaps(
        "swap_attended",
        2,
        sizes,
        ("ctx",),
        (row_attended.reshape(own_width, row_count).T.reshape(ctx_size, tok_count, own_width),),
    )
    attended = jnp.transpose(attended, (1, 0, 2)).reshape(tok_count, width)
    residual = tokens + jnp.dot(attended, attn_full, preferred_element_type=f32)
    normed_two, scale_two = layer_norm(residual)
    normed_mlp = (normed_two * gain_second).astype(bf16)
    (normed_group,) = swaps("gather_normed", 3, sizes, ("gather",), (normed_mlp,))
    group = fsdp_size * tok_count
    normed_group = normed_group.reshape(group, width)
    grad_out_group = grad_out_group.reshape(group, width)

    expanded = jnp.dot(normed_group, in_mine, preferred_element_type=f32)
    pre_act = expanded[:, :own_hidden]
    gate_part = expanded[:, own_hidden:]
    activated = jax.nn.gelu(pre_act, approximate=False)
    product = (activated * gate_part).astype(bf16)
    grad_product = jnp.einsum("td,df->tf", grad_out_group, mlp_turned, preferred_element_type=f32)
    grad_expanded = jnp.concatenate(
        [grad_product * gate_part * gelu_slope(pre_act), grad_product * activated], axis=1
    ).astype(bf16)
    grad_normed_part = jnp.einsum(
        "tf,df->td", grad_expanded, in_mine, preferred_element_type=f32
    ).astype(bf16)
    out_part = jnp.einsum("tf,df->td", product, mlp_turned, preferred_element_type=f32).astype(bf16)

    (grad_normed_parts,) = swaps(
        "swap_grad_normed",
        4,
        sizes,
        ("fsdp",),
        (grad_normed_part.reshape(fsdp_size, tok_count, width),),
    )
    grad_normed_mlp = jnp.sum(grad_normed_parts.astype(f32), axis=0)

    normed_halves = normed_group.reshape(group, line, 2, block_rows)
    grad_out_halves = grad_out_group.reshape(group, line, 2, block_rows)

    def mlp_grads(side):
        left = pick(normed_halves, side, 2).reshape(group, line * block_rows)
        right = pick(grad_out_halves, side, 2).reshape(group, line * block_rows)
        grad_in = jnp.einsum("td,tf->df", left, grad_expanded, preferred_element_type=f32)
        grad_mlp = jnp.einsum("td,tf->df", right, product, preferred_element_type=f32)
        return grad_in, grad_mlp

    swap_pair = [(i, i ^ 1) for i in range(ctx_size)]
    other_in, other_mlp = mlp_grads(1 - parity)
    other_in = lax.ppermute(other_in.astype(bf16), "ctx", swap_pair)
    other_mlp = lax.ppermute(other_mlp.astype(bf16), "ctx", swap_pair)
    mine_in, mine_mlp = mlp_grads(parity)
    sum_in = (mine_in + other_in.astype(f32)).reshape(line, block_rows, 2 * own_hidden)
    sum_mlp = (mine_mlp + other_mlp.astype(f32)).reshape(line, block_rows, own_hidden)

    def line_sum(blocks):
        total = pick(blocks, pos, 0)
        half = blocks.astype(bf16)
        for k in reversed(range(1, line)):
            moved = lax.ppermute(
                pick(half, pos ^ k, 0), "ctx", [(i, i ^ (2 * k)) for i in range(ctx_size)]
            )
            total = total + moved.astype(f32)
        return total.astype(bf16)

    grad_in_block = line_sum(sum_in)
    grad_mlp_block = line_sum(sum_mlp)

    grad_gain_two = jnp.sum(grad_normed_mlp * normed_two, axis=0)
    grad_residual = cotangent[0].astype(f32) + norm_back(
        grad_normed_mlp * gain_second, normed_two, scale_two
    )
    residual_half = grad_residual.astype(bf16)
    grad_attended = jnp.einsum(
        "te,de->td", residual_half, attn_full, preferred_element_type=f32
    ).astype(bf16)
    row_grad, residual_cols, attended_group = swaps(
        "swap_grad_attended",
        5,
        sizes,
        ("ctx", "fsdp", "gather"),
        (
            jnp.transpose(grad_attended.reshape(tok_count, ctx_size, own_width), (1, 0, 2)),
            jnp.transpose(residual_half.reshape(tok_count, fsdp_size, own_out), (1, 0, 2)),
            attended,
        ),
    )
    grad_attn_part = jnp.einsum(
        "td,te->de",
        attended_group.reshape(group, width),
        residual_cols.reshape(group, own_out),
        preferred_element_type=f32,
    ).reshape(line, 2, block_rows, own_out)
    row_grad_cols = row_grad.reshape(row_count, own_width).T.reshape(
        own_heads, head_size, row_count
    )
    grad_query, grad_key, grad_value = attend_grads(
        query_cols,
        key_cols,
        value_cols,
        seg_col,
        seg_row,
        log_total,
        row_grad_cols,
        row_attended,
        scale,
    )
    grad_proj_cols = (
        jnp.stack(
            [
                unrotate_cols(grad_query, cosine, sine),
                unrotate_cols(grad_key, cosine, sine),
                grad_value,
            ],
            axis=0,
        )
        .astype(bf16)
        .reshape(3 * own_width, row_count)
    )
    row_grad_normed = jnp.einsum("de,et->td", qkv_mine, grad_proj_cols, preferred_element_type=f32)
    grad_gain_part = jnp.sum(row_grad_normed * row_normed, axis=0)
    gain_columns = jnp.pad(
        jnp.stack([grad_gain_part, grad_gain_two], axis=1), ((0, 0), (0, LANES - 2))
    )
    qkv_terms = jnp.concatenate(
        [
            jnp.einsum("td,et->de", row_normed_attn, grad_proj_cols, preferred_element_type=f32),
            gain_columns,
        ],
        axis=1,
    ).astype(bf16)
    qkv_width = 3 * own_width + LANES
    qkv_terms = jnp.transpose(
        qkv_terms.reshape(ctx_size, fsdp_size, weight_rows, qkv_width), (1, 0, 2, 3)
    )
    row_grad_blocks = row_grad_normed.reshape(line, 2, tok_count, width)
    row_grad_half = row_grad_blocks.astype(bf16)
    grad_attn_half = grad_attn_part.astype(bf16)
    row_other, attn_other, qkv_got_terms, out_parts = pair_stage(
        6,
        sizes,
        (row_grad_half, grad_attn_half),
        (qkv_terms, out_part.reshape(fsdp_size, tok_count, width)),
    )
    block_out = (residual + jnp.sum(out_parts.astype(f32), axis=0)).astype(bf16)
    row_sum = (pick(row_grad_half, parity, 1).astype(f32) + row_other.astype(f32)).astype(bf16)
    attn_sum = (pick(grad_attn_half, parity, 1).astype(f32) + attn_other.astype(f32)).astype(bf16)
    qkv_half = jnp.sum(qkv_got_terms.astype(f32), axis=0).astype(bf16)
    row_lines, attn_lines, qkv_lines = line_stage(7, sizes, (row_sum, attn_sum), (qkv_half,))
    grad_normed_attn = jnp.sum(row_lines.astype(f32), axis=0)
    grad_attn_block = jnp.sum(attn_lines.astype(f32), axis=0).astype(bf16)
    grad_tokens = (
        grad_residual + norm_back(grad_normed_attn * gain_first, normed_one, scale_one)
    ).astype(bf16)
    grad_qkv_rows = jnp.transpose(
        qkv_lines[:, :, : 3 * own_width].astype(f32).reshape(ctx_size, weight_rows, 3, own_width),
        (1, 2, 0, 3),
    ).reshape(weight_rows, 3 * width)
    gain_sums = jnp.sum(qkv_lines[:, :, 3 * own_width : 3 * own_width + 2].astype(f32), axis=0)

    in_got, mlp_got, attn_got = swaps(
        "swap_weight_grads",
        8,
        sizes,
        ("fsdp", "fsdp", "fsdp"),
        (
            grad_in_block.reshape(fsdp_size, weight_rows, 2 * own_hidden),
            grad_mlp_block.reshape(fsdp_size, weight_rows, own_hidden),
            grad_attn_block.reshape(fsdp_size, weight_rows, own_out),
        ),
    )
    grad_in_rows = jnp.transpose(
        in_got.astype(f32).reshape(fsdp_size, weight_rows, 2, own_hidden), (1, 2, 0, 3)
    ).reshape(weight_rows, 2 * hidden_units)
    grad_mlp_cols = jnp.transpose(mlp_got.astype(f32), (0, 2, 1)).reshape(hidden_units, weight_rows)
    grad_attn_rows = jnp.transpose(attn_got.astype(f32), (1, 0, 2)).reshape(weight_rows, width)
    return (
        block_out[None],
        grad_tokens[None],
        grad_qkv_rows,
        grad_attn_rows,
        grad_in_rows,
        grad_mlp_cols,
        gain_sums[:, 0],
        gain_sums[:, 1],
    )


def solution(mesh):
    in_specs = (
        P("fsdp", "ctx", None),
        P("fsdp", "ctx"),
        P(("ctx", "fsdp")),
        P(("ctx", "fsdp"), None),
        P(("ctx", "fsdp"), None),
        P(("ctx", "fsdp")),
        P(("ctx", "fsdp"), None),
        P(None, ("ctx", "fsdp")),
        P("fsdp", "ctx", None),
    )
    out_specs = (
        P("fsdp", "ctx", None),
        P("fsdp", "ctx", None),
        P(("ctx", "fsdp"), None),
        P(("ctx", "fsdp"), None),
        P(("ctx", "fsdp"), None),
        P(None, ("ctx", "fsdp")),
        P(("ctx", "fsdp")),
        P(("ctx", "fsdp")),
    )
    step = functools.partial(body, mesh.shape["ctx"], mesh.shape["fsdp"])
    return jax.shard_map(step, mesh=mesh, in_specs=in_specs, out_specs=out_specs, check_vma=False)
```

time: 488 us -> 470 us (0.963); the launches traced: 486 us -> 461 us
  waiting for transfers between devices: 281 us -> 25.3 us
  Pallas kernels: 31 us -> 251 us
  local copies, waits for them, and re-layouts: 23.7 us -> 93 us
  blocking collectives: 58.7 us -> 0 us
  other arithmetic: 17.5 us -> 41.2 us
  starting transfers between devices: 26.1 us -> 8.79 us
  between operations: 14.6 us -> 1.77 us
  matrix products: 34 us -> 40 us
    pallas_call x1 -> x8, Pallas kernels: 11.6 us -> 232 us  [exchange(): pl.pallas_call(kernel, in_specs=[anywhere] * len(operands), out_specs=[an...]
    all_to_all x4 -> x0, waiting for transfers between devices: 174 us -> none  [the longest x1 96.5 us: body(): lax.all_to_all(jnp.broadcast_to(jnp.concatenate([inputs[0], seg_block], a...]
    reduce_scatter x1 -> x0, waiting for transfers between devices: 106 us -> none  [body(): lax.psum_scatter(weight_grads(((attended, residual_half), (normed_mlp, gr...]
    all_to_all x2 -> x0, blocking collectives: 58.7 us -> none  [the longest x1 44.8 us: body(): lax.all_to_all(qkv_terms, everyone, 0, 0, tiled=True)]
    dynamic_slice x0 -> x14, local copies, waits for them, and re-layouts: none -> 26.9 us  [pick(): return lax.dynamic_index_in_dim(array, index, axis, keepdims=False)]
    all_to_all x4 -> x0, starting transfers between devices: 26.1 us -> none  [the longest x1 7.91 us: body(): lax.all_to_all(row_grad_normed.astype(jnp.bfloat16).reshape(ctx_size, tok...]
    ppermute x0 -> x8, waiting for transfers between devices: none -> 25.3 us  [the longest x6 25.3 us: line_sum(): lax.ppermute(pick(half, pos ^ k, 0), 'ctx', [(i, i ^ 2 * k) for i in rang...]
    unnamed x49 -> x123, local copies, waits for them, and re-layouts: 5.72 us -> 21.4 us
  transfers between devices with their start and end apart: 6 -> 8, of which waited for: 5 -> 2; matrix products, arithmetic and copies ran while one was open for 8% -> 25% of each run, Pallas kernels for 4% -> 24%
where the time goes in v1:
time: 470 us; the launch traced here: 461 us
  Pallas kernels  251 us (53%)
  local copies, waits for them, and re-layouts  93 us (20%)
  other arithmetic  41.2 us (9%)
  matrix products  40 us (9%)
  waiting for transfers between devices  25.3 us (5%)
  starting transfers between devices  8.79 us (2%)
    pallas_call x8, Pallas kernels, exchange(): pl.pallas_call(kernel, in_specs=[anywhere] * len(operands), out_specs=[an...  232 us
    dynamic_slice x14, local copies, waits for them, and re-layouts, pick(): return lax.dynamic_index_in_dim(array, index, axis, keepdims=False)  26.9 us
    ppermute x6, waiting for transfers between devices, line_sum(): lax.ppermute(pick(half, pos ^ k, 0), 'ctx', [(i, i ^ 2 * k) for i in rang...  25.3 us
    unnamed x123, local copies, waits for them, and re-layouts  21.4 us
    pallas_call x1, Pallas kernels, attend(): pl.pallas_call(lambda *refs: attend_kernel(scale, *refs), grid=(heads, ro...  10 us
    pallas_call x1, Pallas kernels, attend_grads(): pl.pallas_call(lambda *refs: attend_grad_kernel(scale, *refs), grid=(head...  9.53 us
  transfers between devices with their start and end apart: 8, of which 2 were waited for; matrix products, arithmetic and copies ran while one was open for 25% of the time, Pallas kernels for 24%

profile of v1, /device:TPU:11, one launch (start us, length us, event | category | flops | bytes accessed | tf_op | source)
XLA Modules:
  0.0 461.1 jit_solution(11494432944235938117)
XLA Ops:
  7.8 93.4 %gather_all.1 = (bf16[8,128,1024]{2,1,0:T(8,128)(2,1)}, f32[8,8,128]{2,1,0:T(8,128)}, bf16[8,4,32,512]{3,2,1,0:T(8,128)(2,1)}, bf16[8,2,2,32,1024]{4,3,2,1,0:T(8...) custom-call(bf16[128,1024]{1,0:T(8,128)(2,1)} %bitcast.184, ...), custom_call_target="tpu_custom_call" | custom-call | tf_op jit(solution)/shard_map/gather_all/pallas_call | solution.py:406
  102.4 2.1 convert_reduce_fusion
  113.1 10.0 %attend.1 = (bf16[2,64,1024]{2,1,0:T(8,128)(2,1)}, f32[2,1024,1]{2,1,0:T(8,128)}) custom-call(bf16[2,64,1024]{2,1,0:T(8,128)(2,1)} %get-tuple-element.89.refs_0_, bf16[2,64,1024]{2,1,0:T(8,128)(2,1)} %get-tuple-element.88.refs_1_, bf16[2,64,1024]{2,1,0:T(8,128)(2,1)} %bitcast.196, f32[1024,1]{1,0:T(8,128)} %copy.157.refs_3_, f32[1,1024]{1,0:T(1,128)} %get-tuple-element.98.refs_4_), custom_call_target="tpu_custom_call" | custom-call | tf_op jit(solution)/shard_map/attend/pallas_call | solution.py:139
  123.2 1.8 copy.158
  125.0 8.0 %swap_attended.1 = bf16[8,128,128]{2,1,0:T(8,128)(2,1)} custom-call(bf16[8,128,128]{2,1,0:T(8,128)(2,1)} %bitcast.215), custom_call_target="tpu_custom_call" | custom-call | tf_op jit(solution)/shard_map/swap_attended/pallas_call | solution.py:406
  132.9 2.2 fusion.64
  136.3 14.8 %gather_normed.1 = bf16[4,128,1024]{2,1,0:T(8,128)(2,1)} custom-call(bf16[128,1024]{1,0:T(8,128)(2,1)} %multiply_convert_fusion.4.refs_0_), custom_call_target="tpu_custom_call" | custom-call | tf_op jit(solution)/shard_map/gather_normed/pallas_call | solution.py:406
  151.0 2.6 reshape_reshape.6
  153.6 5.0 %constant_dynamic-slice_fusion.11 = (bf16[512,4,1,128]{3,2,1,0:T(2,128)(2,1)}, bf16[512,4,1,128]{3,2,1,0:T(2,128)(2,1)}) fusion(bf16[512,4,2,128]{3,2,1,0:T(2,128)(2,1)} %reshape_reshape.6, s32[]{:T(128)S(6)} %select_n.45, s32[]{:T(128)S(6)} %select_n.46), kind=kLoop, calls=%fused_computation.141 | loop fusion | bytes 2097160 | tf_op jit(solution)/shard_map/jit(dynamic_index_in_dim)/dynamic_slice | solution.py:609
  158.6 3.5 copy.197
  162.1 3.9 fusion.65
  166.0 5.1 %multiply_convert_fusion.2 = (bf16[512,656]{0,1:T(8,128)(2,1)}, f32[512,656]{0,1:T(8,128)S(1)}, bf16[512,656]{0,1:T(8,128)(2,1)S(1)}, f32[512,656]{0,1:T(8,128)S(1)}) fusion(f32[512,1312]{0,1:T(8,128)S(1)} %fusion.65, bf16[512,1024]{1,0:T(8,128)(2,1)S(1)} %bitcast.208, bf16[1024,656]{1,0:T(8,128)(2,1)S(1)} %bitcast.250), kind=kOutput, calls=%fused_computation.33 | convolution fusion | flops 713728000 | bytes 9109504 | tf_op jit(solution)/shard_map/td,df->tf/dot_general | solution.py:709
  172.5 2.0 convolution_convert_fusion
  175.1 2.9 reshape_reshape.7
  178.0 5.1 %constant_dynamic-slice_fusion.4 = (bf16[512,4,1,128]{3,2,1,0:T(2,128)(2,1)}, bf16[512,4,1,128]{3,2,1,0:T(2,128)(2,1)}) fusion(bf16[512,4,2,128]{3,2,1,0:T(2,128)(2,1)} %reshape_reshape.7, s32[]{:T(128)S(6)} %select_n.46, s32[]{:T(128)S(6)} %select_n.45), kind=kLoop, calls=%fused_computation.134 | loop fusion | bytes 2097160 | tf_op jit(solution)/shard_map/jit(dynamic_index_in_dim)/dynamic_slice | solution.py:609
  183.1 3.5 copy.199
  186.6 2.7 convolution_convert_fusion.3
  190.2 4.7 %convolution_convert_fusion.2 = bf16[512,1024]{1,0:T(8,128)(2,1)} fusion(bf16[1024,1312]{1,0:T(8,128)(2,1)} %bitcast.248, bf16[512,656]{0,1:T(8,128)(2,1)S(1)} %multiply_convert_fusion.3, bf16[512,656]{0,1:T(8,128)(2,1)S(1)} %copy-done.20), kind=kOutput, calls=%fused_computation.20 | convolution fusion | flops 1378942976 | bytes 5079040 | tf_op jit(solution)/shard_map/tf,df->td/dot_general | solution.py:713
  194.9 15.4 %swap_grad_normed.1 = bf16[4,128,1024]{2,1,0:T(8,128)(2,1)} custom-call(bf16[4,128,1024]{2,1,0:T(8,128)(2,1)} %bitcast.211), custom_call_target="tpu_custom_call" | custom-call | tf_op jit(solution)/shard_map/swap_grad_normed/pallas_call | solution.py:406
  210.3 1.5 convert_reduce_fusion.3
  214.5 1.5 convolution_convert_fusion.5
  216.0 1.8 copy.162
  217.8 1.7 copy_bitcast_fusion.2.refs_2_
  219.5 3.7 convolution_convert_fusion.1
  223.8 1.8 copy.160
  225.6 1.8 copy.161
  227.4 1.8 copy.163
  229.2 16.1 %swap_grad_attended.1 = (bf16[8,128,128]{2,1,0:T(8,128)(2,1)}, bf16[4,128,256]{2,1,0:T(8,128)(2,1)}, bf16[4,128,1024]{2,1,0:T(8,128)(2,1)}) custom-call(bf16[8,128,128]{2,1,0:T(8,128)(2,1)} %bitcast.205, bf16[4,128,256]{2,1,0:T(8,128)(2,1)} %bitcast.206, bf16[128,1024]{1,0:T(8,128)(2,1)} %copy_bitcast_fusion.2.refs_2_), custom_call_target="tpu_custom_call" | custom-call | tf_op jit(solution)/shard_map/swap_grad_attended/pallas_call | solution.py:406
  245.3 1.8 copy.164
  247.1 9.5 %attend_grads.1 = (f32[2,64,1024]{2,1,0:T(8,128)}, f32[2,64,1024]{2,1,0:T(8,128)}, f32[2,64,1024]{2,1,0:T(8,128)}) custom-call(bf16[2,64,1024]{2,1,0:T(8,128)(2,1)} %get-tuple-element.89.refs_0_, bf16[2,64,1024]{2,1,0:T(8,128)(2,1)} %get-tuple-element.88.refs_1_, bf16[2,64,1024]{2,1,0:T(8,128)(2,1)} %bitcast.197, f32[1024,1]{1,0:T(8,128)} %copy.157.refs_3_, ...), custom_call_target="tpu_custom_call" | custom-call | tf_op jit(solution)/shard_map/attend_grads/pallas_call | solution.py:159
  256.6 1.4 broadcast_multiply_fusion.1
  260.8 3.6 multiply_reduce_fusion
  264.3 2.5 copy.166
  266.9 1.7 convolution_convert_fusion.4
  270.2 2.0 multiply_convert_fusion
  272.2 2.9 copy.168
  277.0 1.6 copy.201
  279.6 2.4 fusion.4
  283.1 33.9 %pair_stage.1 = (bf16[4,128,1024]{2,1,0:T(8,128)(2,1)}, bf16[4,128,256]{2,1,0:T(8,128)(2,1)}, bf16[4,8,32,512]{3,2,1,0:T(8,128)(2,1)}, bf16[4,128,1024]{2,1,0:T(8,128)(2,1)}) custom-call(bf16[4,2,128,1024]{3,2,1,0:T(8,128)(2,1)} %bitcast.188, bf16[4,2,128,256]{3,2,1,0:T(8,128)(2,1)} %copy.172.refs_1_, bf16[4,8,32,512]{3,2,1,0:T(8,128)(2,1)} %maximum_bitcast_fusion.refs_2_, ...), custom_call_target="tpu_custom_call" | custom-call | tf_op jit(solution)/shard_map/pair_stage/pallas_call | solution.py:406
  317.1 2.7 fusion.1.refs_0_
  320.5 2.2 reduce_sum.180.refs_2_
  322.7 37.4 %line_stage.1 = (bf16[4,128,1024]{2,1,0:T(8,128)(2,1)}, bf16[4,128,256]{2,1,0:T(8,128)(2,1)}, bf16[8,32,512]{2,1,0:T(8,128)(2,1)}) custom-call(bf16[4,128,1024]{2,1,0:T(8,128)(2,1)} %fusion.1.refs_0_, bf16[4,128,256]{2,1,0:T(8,128)(2,1)} %fusion.46.refs_1_, bf16[8,32,512]{2,1,0:T(8,128)(2,1)} %reduce_sum.180.refs_2_), custom_call_target="tpu_custom_call" | custom-call | tf_op jit(solution)/shard_map/line_stage/pallas_call | solution.py:406
  360.1 1.7 slice_convert_fusion.2
  361.8 1.5 convert_reduce_fusion.5
  363.3 1.5 convert_reduce_fusion.1
  369.3 2.3 copy.196
  371.6 2.4 copy.198
  375.4 1.5 convert_reduce_fusion.2
  378.7 1.6 convert_add_fusion.2
  384.1 2.6 collective-permute-start.7
  389.6 3.7 convert_add_fusion
  393.4 2.9 reshape.307
  396.7 3.2 constant_dynamic-slice_fusion.8
  399.9 2.8 copy.180
  402.8 2.4 collective-permute-start.3
  405.1 2.8 copy.179
  408.0 1.7 copy.178
  410.8 2.0 fusion.49
  414.3 15.2 %collective-permute-done.2 = bf16[128,1312]{1,0:T(8,128)(2,1)} collective-permute-done((bf16[128,1312]{1,0:T(8,128)(2,1)}, bf16[128,1312]{1,0:T(8,128)(2,1)}, u32[]{:S(2)}, u32[]{:S(2)}) %collective-permute-start.2) | collective-permute-done | bytes 335904 | tf_op jit(solution)/shard_map/ppermute | solution.py:749
  429.5 10.1 %collective-permute-done.1 = bf16[128,1312]{1,0:T(8,128)(2,1)} collective-permute-done((bf16[128,1312]{1,0:T(8,128)(2,1)}, bf16[128,1312]{1,0:T(8,128)(2,1)}, u32[]{:S(2)}, u32[]{:S(2)}) %collective-permute-start.1) | collective-permute-done | bytes 335904 | tf_op jit(solution)/shard_map/ppermute | solution.py:749
  439.6 2.1 fusion.25
  441.7 12.7 %swap_weight_grads.1 = (bf16[4,32,1312]{2,1,0:T(8,128)(2,1)}, bf16[4,32,656]{2,1,0:T(8,128)(2,1)}, bf16[4,32,256]{2,1,0:T(8,128)(2,1)}) custom-call(bf16[4,32,1312]{2,1,0:T(8,128)(2,1)} %bitcast.204, bf16[4,32,656]{2,1,0:T(8,128)(2,1)} %bitcast.222, bf16[4,32,256]{2,1,0:T(8,128)(2,1)} %bitcast.232), custom_call_target="tpu_custom_call" | custom-call | tf_op jit(solution)/shard_map/swap_weight_grads/pallas_call | solution.py:406
  455.9 1.7 reshape.339
  458.2 1.5 reshape.329
  (210 shorter events, 54.0 us)
Async XLA Ops:
  0.6 2.8 copy-start.24
  3.2 2.2 copy-start.28
  102.2 2.3 copy-start
  102.4 3.4 copy-start.30
  102.4 33.0 %copy-start.34 = (f32[1,1024]{1,0:T(1,128)}, f32[1,1024]{1,0:T(1,128)S(1)}, u32[]{:S(2)}) copy-start(f32[1,1024]{1,0:T(1,128)S(1)} %get-tuple-element.100) | copy-start | bytes 12292
  104.5 1.3 copy-start.38
  104.5 2.0 copy-start.41
  105.8 0.7 copy-start.43
  105.8 1.2 copy-start.36
  112.0 1.1 copy-start.5
  112.1 1.1 copy-start.7
  113.1 19.8 %copy-start.1 = (bf16[1,128,1024]{2,1,0:T(8,128)(2,1)S(1)}, bf16[1,128,1024]{2,1,0:T(8,128)(2,1)}, u32[]{:S(2)}) copy-start(bf16[1,128,1024]{2,1,0:T(8,128)(2,1)} %param.9) | copy-start | bytes 786436
  135.2 18.4 %copy-start.45 = (f32[128]{0:T(128)}, f32[128]{0:T(128)S(1)}, u32[]{:S(2)}) copy-start(f32[128]{0:T(128)S(1)} %broadcast_multiply_fusion.8) | copy-start | bytes 1540
  135.4 18.2 %copy-start.47 = (f32[128]{0:T(128)}, f32[128]{0:T(128)S(1)}, u32[]{:S(2)}) copy-start(f32[128]{0:T(128)S(1)} %add_rsqrt_fusion.2) | copy-start | bytes 1540
  162.1 3.9 copy-start.15
  162.1 3.9 copy-start.56
  171.2 0.9 copy-start.19
  171.2 1.3 copy-start.23
  174.4 215.2 %collective-permute-start = (bf16[512,1312]{0,1:T(8,128)(2,1)}, bf16[512,1312]{0,1:T(8,128)(2,1)}, u32[]{:S(2)}, u32[]{:S(2)}) collective-permute-start(bf16[512,1312]{0,1:T(8,128)(2,1)} %convolution_convert_fusion), channel_id=1, source_target_pairs={{0,4},{4,0},{8,12},{12,8},{16,20},{20,16},{24,28},{28,24},{1,5},{5... | collective-permute-start | bytes 4030472 | tf_op jit(solution)/shard_map/ppermute | solution.py:739
  186.6 3.6 copy-start.20
  189.3 189.4 %collective-permute-start.4 = (bf16[512,656]{0,1:T(8,128)(2,1)}, bf16[512,656]{0,1:T(8,128)(2,1)}, u32[]{:S(2)}, u32[]{:S(2)}) collective-permute-start(bf16[512,656]{0,1:T(8,128)(2,1)} %convolution_convert_fusion.3), channel_id=1, source_target_pairs={{0,4},{4,0},{8,12},{12,8},{16,20},{20,16},{24,28},{28,24},{1,5},{5... | collective-permute-start | bytes 2015240 | tf_op jit(solution)/shard_map/ppermute | solution.py:740
  210.3 1.5 copy-start.35
  210.3 1.5 copy-start.46
  210.3 1.5 copy-start.48
  210.3 2.3 copy-start.16
  211.9 2.6 copy-start.2
  213.8 0.7 copy-start.6
  258.0 1.0 copy-start.8
  258.0 1.1 copy-start.11
  258.0 1.3 copy-start.12
  259.2 1.0 copy-start.22
  259.5 1.3 copy-start.37
  259.5 1.3 copy-start.42
  259.5 1.2 copy-start.44
  260.4 3.9 copy-start.17
  266.8 3.3 copy-start.31
  266.8 3.3 copy-start.39
  266.8 3.3 copy-start.40
  268.6 0.8 copy-start.13
  283.1 33.9 %copy-start.3 = (bf16[1024,1024]{1,0:T(8,128)(2,1)S(1)}, bf16[1024,1024]{1,0:T(8,128)(2,1)}, u32[]{:S(2)}) copy-start(bf16[1024,1024]{1,0:T(8,128)(2,1)} %get-tuple-element.70) | copy-start | bytes 6291460
  317.1 2.7 copy-start.14
  317.1 2.7 copy-start.26
  360.1 4.7 %copy-start.53 = (f32[128]{0:T(128)S(1)}, f32[128]{0:T(128)}, u32[]{:S(2)}) copy-start(f32[128]{0:T(128)} %convert_reduce_fusion.4) | copy-start | bytes 1540
  360.1 5.7 %copy-start.32 = (f32[1,1024]{1,0:T(1,128)S(1)}, f32[1,1024]{1,0:T(1,128)}, u32[]{:S(2)}) copy-start(f32[1,1024]{1,0:T(1,128)} %copy-done.30) | copy-start | bytes 12292
  365.3 0.5 copy-start.51
  366.0 3.3 copy-start.4
  369.3 4.6 %copy-start.25 = (bf16[4,128,256]{2,1,0:T(8,128)(2,1)S(1)}, bf16[4,128,256]{2,1,0:T(8,128)(2,1)}, u32[]{:S(2)}) copy-start(bf16[4,128,256]{2,1,0:T(8,128)(2,1)} %get-tuple-element.54) | copy-start | bytes 786436
  371.6 3.1 copy-start.29
  375.4 2.3 copy-start.10
  375.4 2.3 copy-start.33
  375.4 2.3 copy-start.50
  375.4 2.3 copy-start.52
  375.4 2.3 copy-start.54
  375.4 2.3 copy-start.55
  376.9 1.8 copy-start.18
  382.3 7.4 %copy-start.9 = (bf16[512,4,1,128]{0,3,1,2:T(8,128)(2,1)S(1)}, bf16[512,4,1,128]{0,3,1,2:T(8,128)(2,1)}, u32[]{:S(2)}) copy-start(bf16[512,4,1,128]{0,3,1,2:T(8,128)(2,1)} %copy.196) | copy-start | bytes 1572868
  382.3 7.4 %copy-start.21 = (bf16[512,656]{0,1:T(8,128)(2,1)S(1)}, bf16[512,656]{0,1:T(8,128)(2,1)}, u32[]{:S(2)}) copy-start(bf16[512,656]{0,1:T(8,128)(2,1)} %copy-done.19) | copy-start | bytes 2015236
  384.1 25.5 %collective-permute-start.7 = (bf16[128,656]{1,0:T(8,128)(2,1)}, bf16[128,656]{1,0:T(8,128)(2,1)}, u32[]{:S(2)}, u32[]{:S(2)}) collective-permute-start(bf16[128,656]{1,0:T(8,128)(2,1)} %bitcast.71), channel_id=1, source_target_pairs={{0,8},{4,12},{8,0},{12,4},{16,24},{20,28},{24,16},{28,20},{1,9},{5... | collective-permute-start | bytes 503816 | tf_op jit(solution)/shard_map/ppermute | solution.py:749
  387.6 23.2 %collective-permute-start.6 = (bf16[128,656]{1,0:T(8,128)(2,1)}, bf16[128,656]{1,0:T(8,128)(2,1)}, u32[]{:S(2)}, u32[]{:S(2)}) collective-permute-start(bf16[128,656]{1,0:T(8,128)(2,1)} %bitcast.70), channel_id=1, source_target_pairs={{0,16},{4,20},{8,24},{12,28},{16,0},{20,4},{24,8},{28,12},{1,17},{... | collective-permute-start | bytes 503816 | tf_op jit(solution)/shard_map/ppermute | solution.py:749
  388.5 22.4 %collective-permute-start.5 = (bf16[128,656]{1,0:T(8,128)(2,1)}, bf16[128,656]{1,0:T(8,128)(2,1)}, u32[]{:S(2)}, u32[]{:S(2)}) collective-permute-start(bf16[128,656]{1,0:T(8,128)(2,1)} %bitcast.69), channel_id=1, source_target_pairs={{0,24},{4,28},{8,16},{12,20},{16,8},{20,12},{24,0},{28,4},{1,25},{... | collective-permute-start | bytes 503816 | tf_op jit(solution)/shard_map/ppermute | solution.py:749
  402.8 11.5 %collective-permute-start.3 = (bf16[128,1312]{1,0:T(8,128)(2,1)}, bf16[128,1312]{1,0:T(8,128)(2,1)}, u32[]{:S(2)}, u32[]{:S(2)}) collective-permute-start(bf16[128,1312]{1,0:T(8,128)(2,1)} %bitcast.229), channel_id=1, source_target_pairs={{0,8},{4,12},{8,0},{12,4},{16,24},{20,28},{24,16},{28,20},{1,9},{5... | collective-permute-start | bytes 1007624 | tf_op jit(solution)/shard_map/ppermute | solution.py:749
  407.9 21.5 %collective-permute-start.2 = (bf16[128,1312]{1,0:T(8,128)(2,1)}, bf16[128,1312]{1,0:T(8,128)(2,1)}, u32[]{:S(2)}, u32[]{:S(2)}) collective-permute-start(bf16[128,1312]{1,0:T(8,128)(2,1)} %bitcast.230), channel_id=1, source_target_pairs={{0,16},{4,20},{8,24},{12,28},{16,0},{20,4},{24,8},{28,12},{1,17},{... | collective-permute-start | bytes 1007624 | tf_op jit(solution)/shard_map/ppermute | solution.py:749
  409.6 30.0 %collective-permute-start.1 = (bf16[128,1312]{1,0:T(8,128)(2,1)}, bf16[128,1312]{1,0:T(8,128)(2,1)}, u32[]{:S(2)}, u32[]{:S(2)}) collective-permute-start(bf16[128,1312]{1,0:T(8,128)(2,1)} %bitcast.231), channel_id=1, source_target_pairs={{0,24},{4,28},{8,16},{12,20},{16,8},{20,12},{24,0},{28,4},{1,25},{... | collective-permute-start | bytes 1007624 | tf_op jit(solution)/shard_map/ppermute | solution.py:749
  457.6 2.0 copy-start.27
  (1 other events, 0.5 us)

commit v2 on v1

--- a/solution.py
+++ b/solution.py
@@ -515,24 +515,59 @@
     yield from spread(links, lambda peer: src.at[peer], lambda: out.at[me], lambda peer: out.at[peer])
 
 
-def swaps(name, number, sizes, axes, arrays):
+def send_lines(links, src, out):
+    c, n = links.ctx, links.ctx_size
+    pos = c // 2
+    slots = []
+    for k in reversed(range(1, n // 2)):
+        slot = links.slot()
+        slots.append((slot, k))
+        links.ctx_copy(slot, src.at[pos ^ k], out.at[pos], c ^ (2 * k)).start()
+    yield
+    for slot, k in slots:
+        links.ctx_copy(slot, src.at[pos ^ k], out.at[pos ^ k], c ^ (2 * k)).wait()
+
+
+def send_pairs(links, src, out):
+    c, n = links.ctx, links.ctx_size
+    slots = []
+    for q in range(n // 2):
+        slot = links.slot()
+        slots.append(slot)
+        links.ctx_copy(slot, src.at[q, 1 - c % 2], out.at[q], c ^ 1).start()
+    yield
+    for q, slot in enumerate(slots):
+        links.ctx_copy(slot, src.at[q, 1 - c % 2], out.at[q], c ^ 1).wait()
+
+
+def stage(name, number, sizes, kinds, arrays):
     def tasks(links, ins, outs):
         result = []
         own = []
-        for axis, src, out in zip(axes, ins, outs):
-            me = links.ctx if axis == "ctx" else links.fsdp
-            if axis == "gather":
+        for kind, src, out in zip(kinds, ins, outs):
+            if kind == "pair":
+                result.append(send_pairs(links, src, out))
+            elif kind == "line":
+                pos = links.ctx // 2
+                result.append(send_lines(links, src, out))
+                own.append((src.at[pos], out.at[pos]))
+            elif kind == "gather":
                 result.append(gather_fsdp(links, src, lambda b, out=out: out.at[b]))
-                own.append((src, out.at[me]))
+                own.append((src, out.at[links.fsdp]))
             else:
-                result.append(swap_task(links, axis, src, out))
+                me = links.ctx if kind == "ctx" else links.fsdp
+                result.append(swap_task(links, kind, src, out))
                 own.append((src.at[me], out.at[me]))
-        return result + [local_task(links, own)]
-
-    outs = [
-        (((sizes[1],) if axis == "gather" else ()) + array.shape, array.dtype)
-        for axis, array in zip(axes, arrays)
-    ]
+        return result + ([local_task(links, own)] if own else [])
+
+    outs = []
+    for kind, array in zip(kinds, arrays):
+        shape = array.shape
+        if kind == "pair":
+            shape = shape[:1] + shape[2:]
+        elif kind == "gather":
+            shape = (sizes[1],) + shape
+        outs.append((shape, array.dtype))
     return exchange(
         name,
         number,
@@ -540,69 +575,51 @@
         tasks,
         tuple(arrays),
         outs,
-        over_ctx="ctx" in axes,
-        over_fsdp="fsdp" in axes or "gather" in axes,
-        slots=4 * (sizes[0] + sizes[1]),
-    )
-
-
-def pair_stage(number, sizes, halves, fsdp_arrays):
-    n, fs = sizes
-
-    def tasks(links, ins, outs):
-        c = links.ctx
-        result = []
-        for src, out in zip(ins[: len(halves)], outs):
-            def send(src=src, out=out):
-                slots = []
-                for q in range(n // 2):
-                    slot = links.slot()
-                    slots.append(slot)
-                    links.ctx_copy(slot, src.at[q, 1 - c % 2], out.at[q], c ^ 1).start()
-                yield
-                for q, slot in enumerate(slots):
-                    links.ctx_copy(slot, src.at[q, 1 - c % 2], out.at[q], c ^ 1).wait()
-            result.append(send())
-        own = []
-        for src, out in zip(ins[len(halves) :], outs[len(halves) :]):
-            result.append(swap_task(links, "fsdp", src, out))
-            own.append((src.at[links.fsdp], out.at[links.fsdp]))
-        return result + [local_task(links, own)]
-
-    outs = [((array.shape[0],) + array.shape[2:], array.dtype) for array in halves]
-    outs += [(array.shape, array.dtype) for array in fsdp_arrays]
-    return exchange("pair_stage", number, sizes, tasks, tuple(halves) + tuple(fsdp_arrays), outs)
-
-
-def line_stage(number, sizes, lines, ctx_arrays):
-    n, fs = sizes
-
-    def tasks(links, ins, outs):
-        c = links.ctx
-        pos = c // 2
-        result = []
-        own = []
-        for src, out in zip(ins[: len(lines)], outs):
-            own.append((src.at[pos], out.at[pos]))
-            def send(src=src, out=out):
-                slots = []
-                for k in reversed(range(1, n // 2)):
-                    slot = links.slot()
-                    slots.append((slot, k))
-                    links.ctx_copy(slot, src.at[pos ^ k], out.at[pos], c ^ (2 * k)).start()
-                yield
-                for slot, k in slots:
-                    links.ctx_copy(slot, src.at[pos ^ k], out.at[pos ^ k], c ^ (2 * k)).wait()
-            result.append(send())
-        for src, out in zip(ins[len(lines) :], outs[len(lines) :]):
-            result.append(swap_task(links, "ctx", src, out))
-            own.append((src.at[c], out.at[c]))
-        return result + [local_task(links, own)]
-
-    outs = [(array.shape, array.dtype) for array in tuple(lines) + tuple(ctx_arrays)]
-    return exchange(
-        "line_stage", number, sizes, tasks, tuple(lines) + tuple(ctx_arrays), outs, over_fsdp=False
-    )
+        over_ctx=any(kind in ("pair", "line", "ctx") for kind in kinds),
+        over_fsdp=any(kind in ("fsdp", "gather") for kind in kinds),
+        slots=len(arrays) * 2 * (sizes[0] + sizes[1]),
+    )
+
+
+def grad_blocks_kernel(side_ref, *refs):
+    left_ref, in_ref, right_ref, mlp_ref = refs[:4]
+    dims = (((0,), (0,)), ((), ()))
+    left = left_ref[...].reshape(in_ref.shape[0], -1)
+    right = right_ref[...].reshape(in_ref.shape[0], -1)
+    grad_in = lax.dot_general(left, in_ref[...], dims, preferred_element_type=jnp.float32)
+    grad_mlp = lax.dot_general(right, mlp_ref[...], dims, preferred_element_type=jnp.float32)
+    if len(refs) == 8:
+        grad_in = grad_in + refs[4][0].astype(jnp.float32)
+        grad_mlp = grad_mlp + refs[5][0].astype(jnp.float32)
+    refs[-2][0] = grad_in.astype(jnp.bfloat16)
+    refs[-1][0] = grad_mlp.astype(jnp.bfloat16)
+
+
+def grad_blocks(side, line, normed, grad_expanded, grad_out, product, received=()):
+    tokens, width = normed.shape
+    rows = width // (2 * line)
+    picked = pl.BlockSpec((tokens, rows), lambda q, side_ref: (0, 2 * q + side_ref[0]))
+    if rows % LANES:
+        picked = pl.BlockSpec((1, tokens, rows), lambda q, side_ref: (2 * q + side_ref[0], 0, 0))
+        normed = jnp.transpose(normed.reshape(tokens, 2 * line, rows), (1, 0, 2))
+        grad_out = jnp.transpose(grad_out.reshape(tokens, 2 * line, rows), (1, 0, 2))
+    wide = [grad_expanded.shape[1], product.shape[1]]
+    whole = [pl.BlockSpec((tokens, w), lambda q, side_ref: (0, 0)) for w in wide]
+    block = [pl.BlockSpec((1, rows, w), lambda q, side_ref: (q, 0, 0)) for w in wide]
+    return pl.pallas_call(
+        grad_blocks_kernel,
+        grid_spec=pltpu.PrefetchScalarGridSpec(
+            num_scalar_prefetch=1,
+            grid=(line,),
+            in_specs=[picked, whole[0], picked, whole[1]] + block[: len(received)],
+            out_specs=block,
+        ),
+        out_shape=[jax.ShapeDtypeStruct((line, rows, w), jnp.bfloat16) for w in wide],
+        cost_estimate=pl.CostEstimate(
+            flops=tokens * width * sum(wide), bytes_accessed=6 * tokens * width, transcendentals=0
+        ),
+        name="grad_blocks",
+    )(side, normed, grad_expanded, grad_out, product, *received)
 
 
 def pick(array, index, axis):
@@ -685,7 +702,7 @@
     value_cols = projected_cols[2].astype(bf16)
     row_attended, log_total = attend(query_cols, key_cols, value_cols, seg_col, seg_row, scale)
 
-    (attended,) = swaps(
+    (attended,) = stage(
         "swap_attended",
         2,
         sizes,
@@ -696,7 +713,7 @@
     residual = tokens + jnp.dot(attended, attn_full, preferred_element_type=f32)
     normed_two, scale_two = layer_norm(residual)
     normed_mlp = (normed_two * gain_second).astype(bf16)
-    (normed_group,) = swaps("gather_normed", 3, sizes, ("gather",), (normed_mlp,))
+    (normed_group,) = stage("gather_normed", 3, sizes, ("gather",), (normed_mlp,))
     group = fsdp_size * tok_count
     normed_group = normed_group.reshape(group, width)
     grad_out_group = grad_out_group.reshape(group, width)
@@ -715,7 +732,7 @@
     ).astype(bf16)
     out_part = jnp.einsum("tf,df->td", product, mlp_turned, preferred_element_type=f32).astype(bf16)
 
-    (grad_normed_parts,) = swaps(
+    (grad_normed_parts,) = stage(
         "swap_grad_normed",
         4,
         sizes,
@@ -724,36 +741,10 @@
     )
     grad_normed_mlp = jnp.sum(grad_normed_parts.astype(f32), axis=0)
 
-    normed_halves = normed_group.reshape(group, line, 2, block_rows)
-    grad_out_halves = grad_out_group.reshape(group, line, 2, block_rows)
-
-    def mlp_grads(side):
-        left = pick(normed_halves, side, 2).reshape(group, line * block_rows)
-        right = pick(grad_out_halves, side, 2).reshape(group, line * block_rows)
-        grad_in = jnp.einsum("td,tf->df", left, grad_expanded, preferred_element_type=f32)
-        grad_mlp = jnp.einsum("td,tf->df", right, product, preferred_element_type=f32)
-        return grad_in, grad_mlp
-
+    side = jnp.reshape(parity, (1,)).astype(jnp.int32)
     swap_pair = [(i, i ^ 1) for i in range(ctx_size)]
-    other_in, other_mlp = mlp_grads(1 - parity)
-    other_in = lax.ppermute(other_in.astype(bf16), "ctx", swap_pair)
-    other_mlp = lax.ppermute(other_mlp.astype(bf16), "ctx", swap_pair)
-    mine_in, mine_mlp = mlp_grads(parity)
-    sum_in = (mine_in + other_in.astype(f32)).reshape(line, block_rows, 2 * own_hidden)
-    sum_mlp = (mine_mlp + other_mlp.astype(f32)).reshape(line, block_rows, own_hidden)
-
-    def line_sum(blocks):
-        total = pick(blocks, pos, 0)
-        half = blocks.astype(bf16)
-        for k in reversed(range(1, line)):
-            moved = lax.ppermute(
-                pick(half, pos ^ k, 0), "ctx", [(i, i ^ (2 * k)) for i in range(ctx_size)]
-            )
-            total = total + moved.astype(f32)
-        return total.astype(bf16)
-
-    grad_in_block = line_sum(sum_in)
-    grad_mlp_block = line_sum(sum_mlp)
+    sent = grad_blocks(1 - side, line, normed_group, grad_expanded, grad_out_group, product)
+    received = [lax.ppermute(blocks, "ctx", swap_pair) for blocks in sent]
 
     grad_gain_two = jnp.sum(grad_normed_mlp * normed_two, axis=0)
     grad_residual = cotangent[0].astype(f32) + norm_back(
@@ -763,7 +754,7 @@
     grad_attended = jnp.einsum(
         "te,de->td", residual_half, attn_full, preferred_element_type=f32
     ).astype(bf16)
-    row_grad, residual_cols, attended_group = swaps(
+    row_grad, residual_cols, attended_group = stage(
         "swap_grad_attended",
         5,
         sizes,
@@ -825,17 +816,42 @@
     row_grad_blocks = row_grad_normed.reshape(line, 2, tok_count, width)
     row_grad_half = row_grad_blocks.astype(bf16)
     grad_attn_half = grad_attn_part.astype(bf16)
-    row_other, attn_other, qkv_got_terms, out_parts = pair_stage(
+    in_sum, mlp_sum = grad_blocks(
+        side, line, normed_group, grad_expanded, grad_out_group, product, received
+    )
+    row_other, attn_other, in_lines, mlp_lines, qkv_got_terms, out_parts = stage(
+        "pair_stage",
         6,
         sizes,
-        (row_grad_half, grad_attn_half),
-        (qkv_terms, out_part.reshape(fsdp_size, tok_count, width)),
+        ("pair", "pair", "line", "line", "fsdp", "fsdp"),
+        (
+            row_grad_half,
+            grad_attn_half,
+            in_sum,
+            mlp_sum,
+            qkv_terms,
+            out_part.reshape(fsdp_size, tok_count, width),
+        ),
     )
     block_out = (residual + jnp.sum(out_parts.astype(f32), axis=0)).astype(bf16)
     row_sum = (pick(row_grad_half, parity, 1).astype(f32) + row_other.astype(f32)).astype(bf16)
     attn_sum = (pick(grad_attn_half, parity, 1).astype(f32) + attn_other.astype(f32)).astype(bf16)
     qkv_half = jnp.sum(qkv_got_terms.astype(f32), axis=0).astype(bf16)
-    row_lines, attn_lines, qkv_lines = line_stage(7, sizes, (row_sum, attn_sum), (qkv_half,))
+    grad_in_block = jnp.sum(in_lines.astype(f32), axis=0).astype(bf16)
+    grad_mlp_block = jnp.sum(mlp_lines.astype(f32), axis=0).astype(bf16)
+    row_lines, attn_lines, qkv_lines, in_got, mlp_got = stage(
+        "line_stage",
+        7,
+        sizes,
+        ("line", "line", "ctx", "fsdp", "fsdp"),
+        (
+            row_sum,
+            attn_sum,
+            qkv_half,
+            grad_in_block.reshape(fsdp_size, weight_rows, 2 * own_hidden),
+            grad_mlp_block.reshape(fsdp_size, weight_rows, own_hidden),
+        ),
+    )
     grad_normed_attn = jnp.sum(row_lines.astype(f32), axis=0)
     grad_attn_block = jnp.sum(attn_lines.astype(f32), axis=0).astype(bf16)
     grad_tokens = (
@@ -847,16 +863,12 @@
     ).reshape(weight_rows, 3 * width)
     gain_sums = jnp.sum(qkv_lines[:, :, 3 * own_width : 3 * own_width + 2].astype(f32), axis=0)
 
-    in_got, mlp_got, attn_got = swaps(
+    (attn_got,) = stage(
         "swap_weight_grads",
         8,
         sizes,
-        ("fsdp", "fsdp", "fsdp"),
-        (
-            grad_in_block.reshape(fsdp_size, weight_rows, 2 * own_hidden),
-            grad_mlp_block.reshape(fsdp_size, weight_rows, own_hidden),
-            grad_attn_block.reshape(fsdp_size, weight_rows, own_out),
-        ),
+        ("fsdp",),
+        (grad_attn_block.reshape(fsdp_size, weight_rows, own_out),),
     )
     grad_in_rows = jnp.transpose(
         in_got.astype(f32).reshape(fsdp_size, weight_rows, 2, own_hidden), (1, 2, 0, 3)

time: 470 us -> 397 us (0.84)
  local copies, waits for them, and re-layouts: 93 us -> 43.8 us
  Pallas kernels: 251 us -> 279 us
  waiting for transfers between devices: 25.3 us -> 0.01 us
  matrix products: 40 us -> 30 us
  starting transfers between devices: 8.79 us -> 1.47 us
  other arithmetic: 41.2 us -> 36 us
    dynamic_slice x14 -> x0, local copies, waits for them, and re-layouts: 26.9 us -> none  [pick(): return lax.dynamic_index_in_dim(array, index, axis, keepdims=False)]
    ppermute x8 -> x2, waiting for transfers between devices: 25.3 us -> 0.01 us  [body(): received = [lax.ppermute(blocks, 'ctx', swap_pair) for blocks in sent]]
    pallas_call x8, Pallas kernels: 232 us -> 248 us  [exchange(): pl.pallas_call(kernel, in_specs=[anywhere] * len(operands), out_specs=[an...]
    unnamed x123 -> x63, local copies, waits for them, and re-layouts: 21.4 us -> 6.5 us
    pallas_call x0 -> x2, Pallas kernels: none -> 10.9 us  [grad_blocks(): pl.pallas_call(grad_blocks_kernel, grid_spec=pltpu.PrefetchScalarGridSpec...]
    dot_general x4 -> x0, matrix products: 10.1 us -> none  [the longest x2 5.71 us: mlp_grads(): jnp.einsum('td,tf->df', left, grad_expanded, preferred_element_type=f32)]
    ppermute x8 -> x2, starting transfers between devices: 8.79 us -> 1.47 us  [body(): received = [lax.ppermute(blocks, 'ctx', swap_pair) for blocks in sent]]
    another operation x2 -> x0, local copies, waits for them, and re-layouts: 5.51 us -> none  [the longest x1 2.94 us: body(): grad_out_halves = grad_out_group.reshape(group, line, 2, block_rows)]
  transfers between devices with their start and end apart: 8 -> 2, of which waited for: 2 -> 0; matrix products, arithmetic and copies ran while one was open for 25% -> 11% of each run, Pallas kernels for 24% -> 11%
where the time goes in v2:
time: 397 us; the launch traced here: 391 us
  Pallas kernels  279 us (70%)
  local copies, waits for them, and re-layouts  43.8 us (11%)
  other arithmetic  36 us (9%)
  matrix products  30 us (8%)
    pallas_call x8, Pallas kernels, exchange(): pl.pallas_call(kernel, in_specs=[anywhere] * len(operands), out_specs=[an...  248 us
    pallas_call x2, Pallas kernels, grad_blocks(): pl.pallas_call(grad_blocks_kernel, grid_spec=pltpu.PrefetchScalarGridSpec...  10.9 us
    pallas_call x1, Pallas kernels, attend(): pl.pallas_call(lambda *refs: attend_kernel(scale, *refs), grid=(heads, ro...  9.99 us
    pallas_call x1, Pallas kernels, attend_grads(): pl.pallas_call(lambda *refs: attend_grad_kernel(scale, *refs), grid=(head...  9.57 us
  transfers between devices with their start and end apart: 2, of which 0 were waited for; matrix products, arithmetic and copies ran while one was open for 11% of the time, Pallas kernels for 11%

profile of v2, /device:TPU:11, one launch (start us, length us, event | category | flops | bytes accessed | tf_op | source)
XLA Modules:
  0.0 391.4 jit_solution(4420265771099904634)
XLA Ops:
  2.1 1.0 copy.174
  3.4 1.6 reshape.263
  5.3 1.0 reshape.264.refs_4_
  8.7 93.4 %gather_all.1 = (bf16[8,128,1024]{2,1,0:T(8,128)(2,1)}, f32[8,8,128]{2,1,0:T(8,128)}, bf16[8,4,32,512]{3,2,1,0:T(8,128)(2,1)}, bf16[8,2,2,32,1024]{4,3,2,1,0:T(8...) custom-call(bf16[128,1024]{1,0:T(8,128)(2,1)} %bitcast.153, ...), custom_call_target="tpu_custom_call" | custom-call | tf_op jit(solution)/shard_map/gather_all/pallas_call | solution.py:406
  102.1 1.1 slice_convert_fusion.1
  103.4 1.9 convert_reduce_fusion
  107.3 1.0 fusion.25
  109.2 1.4 slice_bitcast_fusion
  110.5 1.0 copy.133.refs_3_
  113.0 1.1 fusion.40
  114.0 10.0 %attend.1 = (bf16[2,64,1024]{2,1,0:T(8,128)(2,1)}, f32[2,1024,1]{2,1,0:T(8,128)}) custom-call(bf16[2,64,1024]{2,1,0:T(8,128)(2,1)} %get-tuple-element.89.refs_0_, bf16[2,64,1024]{2,1,0:T(8,128)(2,1)} %get-tuple-element.88.refs_1_, bf16[2,64,1024]{2,1,0:T(8,128)(2,1)} %bitcast.167, f32[1024,1]{1,0:T(8,128)} %copy.133.refs_3_, f32[1,1024]{1,0:T(1,128)} %get-tuple-element.98.refs_4_), custom_call_target="tpu_custom_call" | custom-call | tf_op jit(solution)/shard_map/attend/pallas_call | solution.py:139
  124.0 1.8 copy.134
  125.8 7.5 %swap_attended.1 = bf16[8,128,128]{2,1,0:T(8,128)(2,1)} custom-call(bf16[8,128,128]{2,1,0:T(8,128)(2,1)} %bitcast.183), custom_call_target="tpu_custom_call" | custom-call | tf_op jit(solution)/shard_map/swap_attended/pallas_call | solution.py:406
  133.4 2.2 fusion.54
  135.8 0.9 multiply_convert_fusion.4.refs_0_
  136.7 14.3 %gather_normed.1 = bf16[4,128,1024]{2,1,0:T(8,128)(2,1)} custom-call(bf16[128,1024]{1,0:T(8,128)(2,1)} %multiply_convert_fusion.4.refs_0_), custom_call_target="tpu_custom_call" | custom-call | tf_op jit(solution)/shard_map/gather_normed/pallas_call | solution.py:406
  151.1 4.1 %fusion.55 = f32[512,1312]{1,0:T(8,128)S(1)} fusion(bf16[512,1024]{1,0:T(8,128)(2,1)} %bitcast.150, bf16[1024,1312]{1,0:T(8,128)(2,1)} %bitcast.210), kind=kOutput, calls=%fused_computation.139 | convolution fusion | flops 1375731712 | bytes 6422528 | tf_op jit(solution)/shard_map/dot_general | solution.py:721
  155.1 6.0 %multiply_convert_fusion.2 = (bf16[512,656]{1,0:T(8,128)(2,1)}, f32[512,656]{1,0:T(8,128)S(1)}, bf16[512,656]{1,0:T(8,128)(2,1)S(1)}, f32[512,656]{1,0:T(8,128)S(1)}) fusion(f32[512,1312]{1,0:T(8,128)S(1)} %fusion.55, bf16[512,1024]{1,0:T(8,128)(2,1)S(1)} %bitcast.165, bf16[1024,656]{1,0:T(8,128)(2,1)S(1)} %bitcast.212), kind=kOutput, calls=%fused_computation.25 | convolution fusion | flops 713728000 | bytes 9109504 | tf_op jit(solution)/shard_map/td,df->tf/dot_general | solution.py:726
  161.4 1.6 pad_maximum_fusion.refs_1_
  162.9 5.3 %grad_blocks.2 = (bf16[4,128,1312]{2,1,0:T(8,128)(2,1)}, bf16[4,128,656]{2,1,0:T(8,128)(2,1)}) custom-call(s32[1]{0:T(128)S(6)} %sub.64.side_ref, bf16[512,1024]{1,0:T(8,128)(2,1)} %bitcast.151, bf16[512,1312]{1,0:T(8,128)(2,1)} %pad_maximum_fusion.refs_1_, bf16[512,1024]{1,0:T(8,128)(2,1)} %bitcast.163, bf16[512,656]{1,0:T(8,128)(2,1)} %get-tuple-element.75.refs_3_), custom_call_target="tpu_custom_call" | custom-call | flops 1031798784 | bytes 3145728 | tf_op jit(solution)/shard_map/grad_blocks/pallas_call | solution.py:609
  168.2 2.5 copy.148
  171.3 2.2 copy.149
  173.6 0.8 collective-permute-start.1
  174.4 5.1 %convolution_convert_fusion.1 = bf16[512,1024]{1,0:T(8,128)(2,1)} fusion(bf16[512,1312]{1,0:T(8,128)(2,1)} %pad_maximum_fusion.refs_1_, bf16[1024,1312]{1,0:T(8,128)(2,1)} %bitcast.211), kind=kOutput, calls=%fused_computation.43 | convolution fusion | flops 1376256000 | bytes 5079040 | tf_op jit(solution)/shard_map/tf,df->td/dot_general | solution.py:730
  179.5 15.0 %swap_grad_normed.1 = bf16[4,128,1024]{2,1,0:T(8,128)(2,1)} custom-call(bf16[4,128,1024]{2,1,0:T(8,128)(2,1)} %bitcast.179), custom_call_target="tpu_custom_call" | custom-call | tf_op jit(solution)/shard_map/swap_grad_normed/pallas_call | solution.py:406
  194.5 1.5 convert_reduce_fusion.3
  196.3 1.1 fusion.49
  197.8 1.5 convolution_convert_fusion.3
  199.3 0.8 copy.142
  201.0 1.1 copy.140
  202.2 0.8 copy.141
  203.0 0.9 copy.143
  203.9 19.1 %swap_grad_attended.1 = (bf16[8,128,128]{2,1,0:T(8,128)(2,1)}, bf16[4,128,256]{2,1,0:T(8,128)(2,1)}, bf16[4,128,1024]{2,1,0:T(8,128)(2,1)}) custom-call(bf16[8,128,128]{2,1,0:T(8,128)(2,1)} %bitcast.174, bf16[4,128,256]{2,1,0:T(8,128)(2,1)} %bitcast.175, bf16[128,1024]{1,0:T(8,128)(2,1)} %copy_bitcast_fusion.2.refs_2_), custom_call_target="tpu_custom_call" | custom-call | tf_op jit(solution)/shard_map/swap_grad_attended/pallas_call | solution.py:406
  222.9 1.8 copy.144
  224.7 9.6 %attend_grads.1 = (f32[2,64,1024]{2,1,0:T(8,128)}, f32[2,64,1024]{2,1,0:T(8,128)}, f32[2,64,1024]{2,1,0:T(8,128)}) custom-call(bf16[2,64,1024]{2,1,0:T(8,128)(2,1)} %get-tuple-element.89.refs_0_, bf16[2,64,1024]{2,1,0:T(8,128)(2,1)} %get-tuple-element.88.refs_1_, bf16[2,64,1024]{2,1,0:T(8,128)(2,1)} %bitcast.168, f32[1024,1]{1,0:T(8,128)} %copy.133.refs_3_, ...), custom_call_target="tpu_custom_call" | custom-call | tf_op jit(solution)/shard_map/attend_grads/pallas_call | solution.py:159
  234.3 1.3 broadcast_multiply_fusion.1
  235.7 0.8 copy-done.9
  237.3 1.4 copy-done.26
  238.6 3.0 multiply_reduce_fusion
  241.6 2.3 copy.146
  243.9 1.7 convolution_convert_fusion.2
  245.6 0.8 copy.156.refs_1_
  246.5 2.0 multiply_convert_fusion
  248.4 2.9 copy.152
  251.6 3.3 fusion.19
  255.2 2.4 maximum_bitcast_fusion.refs_4_
  257.6 2.0 convolution_convert_fusion
  259.6 2.2 copy.151.refs_5_
  261.9 2.5 copy.150.refs_4_
  264.4 5.7 %grad_blocks.3 = (bf16[4,128,1312]{2,1,0:T(8,128)(2,1)}, bf16[4,128,656]{2,1,0:T(8,128)(2,1)}) custom-call(s32[1]{0:T(128)} %bitcast.47.side_ref, bf16[512,1024]{1,0:T(8,128)(2,1)} %bitcast.152, bf16[512,1312]{1,0:T(8,128)(2,1)} %pad_maximum_fusion.refs_1_, bf16[512,1024]{1,0:T(8,128)(2,1)} %bitcast.164, bf16[512,656]{1,0:T(8,128)(2,1)} %get-tuple-element.75.refs_3_, ...), custom_call_target="tpu_custom_call" | custom-call | flops 1031798784 | bytes 3145728 | tf_op jit(solution)/shard_map/grad_blocks/pallas_call | solution.py:609
  270.0 53.0 %pair_stage.1 = (bf16[4,128,1024]{2,1,0:T(8,128)(2,1)}, bf16[4,128,256]{2,1,0:T(8,128)(2,1)}, bf16[4,128,1312]{2,1,0:T(8,128)(2,1)}, bf16[4,128,656]{2,1,0:T(8,1...) custom-call(bf16[4,2,128,1024]{3,2,1,0:T(8,128)(2,1)} %bitcast.157, ...), custom_call_target="tpu_custom_call" | custom-call | tf_op jit(solution)/shard_map/pair_stage/pallas_call | solution.py:406
  323.1 2.7 fusion.1.refs_0_
  326.5 2.2 reduce_sum.204.refs_2_
  328.7 1.0 reduce_sum.205
  329.7 2.0 reduce_sum.206
  331.7 39.6 %line_stage.1 = (bf16[4,128,1024]{2,1,0:T(8,128)(2,1)}, bf16[4,128,256]{2,1,0:T(8,128)(2,1)}, bf16[8,32,512]{2,1,0:T(8,128)(2,1)}, bf16[4,32,1312]{2,1,0:T(8,128)(2,1)}, bf16[4,32,656]{2,1,0:T(8,128)(2,1)}) custom-call(bf16[4,128,1024]{2,1,0:T(8,128)(2,1)} %fusion.1.refs_0_, bf16[4,128,256]{2,1,0:T(8,128)(2,1)} %fusion.43.refs_1_, ...), custom_call_target="tpu_custom_call" | custom-call | tf_op jit(solution)/shard_map/line_stage/pallas_call | solution.py:406
  371.3 1.0 slice_convert_fusion.2
  372.3 0.9 convert_reduce_fusion.5
  373.3 1.5 convert_reduce_fusion.2
  377.8 6.3 %swap_weight_grads.1 = bf16[4,32,256]{2,1,0:T(8,128)(2,1)} custom-call(bf16[4,32,256]{2,1,0:T(8,128)(2,1)} %bitcast.195), custom_call_target="tpu_custom_call" | custom-call | tf_op jit(solution)/shard_map/swap_weight_grads/pallas_call | solution.py:406
  384.2 0.9 convert_bitcast_fusion.1
  387.0 1.4 reshape.305
  388.8 1.0 reshape.307
  390.4 1.0 fusion.45
  (121 shorter events, 19.3 us)
Async XLA Ops:
  3.1 3.3 copy-start.24
  102.1 3.3 copy-start
  106.1 1.2 copy-start.25
  112.3 0.7 copy-start.6
  112.3 1.8 copy-start.8
  114.0 19.3 %copy-start.1 = (bf16[1,128,1024]{2,1,0:T(8,128)(2,1)S(1)}, bf16[1,128,1024]{2,1,0:T(8,128)(2,1)}, u32[]{:S(2)}) copy-start(bf16[1,128,1024]{2,1,0:T(8,128)(2,1)} %param.9) | copy-start | bytes 786436
  151.0 4.1 %copy-start.4 = (bf16[4,128,1024]{2,1,0:T(8,128)(2,1)S(1)}, bf16[4,128,1024]{2,1,0:T(8,128)(2,1)}, u32[]{:S(2)}) copy-start(bf16[4,128,1024]{2,1,0:T(8,128)(2,1)} %get-tuple-element.44) | copy-start | bytes 3145732
  151.0 4.1 %copy-start.27 = (bf16[8,4,32,656]{3,2,1,0:T(8,128)(2,1)S(1)}, bf16[8,4,32,656]{3,2,1,0:T(8,128)(2,1)}, u32[]{:S(2)}) copy-start(bf16[8,4,32,656]{3,2,1,0:T(8,128)(2,1)} %get-tuple-element.45) | copy-start | bytes 4030468
  170.7 91.1 %collective-permute-start = (bf16[4,128,1312]{1,2,0:T(8,128)(2,1)}, bf16[4,128,1312]{1,2,0:T(8,128)(2,1)}, u32[]{:S(2)}, u32[]{:S(2)}) collective-permute-start(bf16[4,128,1312]{1,2,0:T(8,128)(2,1)} %copy.148), channel_id=1, source_target_pairs={{0,4},{4,0},{8,12},{12,8},{16,20},{20,16},{24,28},{28,24},{1,5},{5... | collective-permute-start | bytes 4030472 | tf_op jit(solution)/shard_map/ppermute | solution.py:747
  173.6 86.0 %collective-permute-start.1 = (bf16[4,128,656]{1,2,0:T(8,128)(2,1)}, bf16[4,128,656]{1,2,0:T(8,128)(2,1)}, u32[]{:S(2)}, u32[]{:S(2)}) collective-permute-start(bf16[4,128,656]{1,2,0:T(8,128)(2,1)} %copy.149), channel_id=1, source_target_pairs={{0,4},{4,0},{8,12},{12,8},{16,20},{20,16},{24,28},{28,24},{1,5},{5... | collective-permute-start | bytes 2015240 | tf_op jit(solution)/shard_map/ppermute | solution.py:747
  194.5 1.8 copy-start.16
  196.0 1.8 copy-start.2
  197.8 2.4 copy-start.10
  200.2 2.8 copy-start.17
  224.7 9.6 %copy-start.7 = (f32[64,1024]{1,0:T(8,128)S(1)}, f32[64,1024]{1,0:T(8,128)}, u32[]{:S(2)}) copy-start(f32[64,1024]{1,0:T(8,128)} %copy-done.6) | copy-start | bytes 786436
  235.6 1.0 copy-start.9
  235.6 1.1 copy-start.12
  235.6 1.3 copy-start.13
  235.7 1.4 copy-start.19
  237.1 1.5 copy-start.26
  237.3 4.4 %copy-start.18 = (bf16[3,2,64,1024]{3,2,1,0:T(8,128)(2,1)}, bf16[3,2,64,1024]{3,2,1,0:T(8,128)(2,1)S(1)}, u32[]{:S(2)}) copy-start(bf16[3,2,64,1024]{3,2,1,0:T(8,128)(2,1)S(1)} %maximum_convert_fusion) | copy-start | bytes 2359300
  254.9 2.7 copy-start.5
  255.2 2.4 copy-start.28
  270.0 53.0 %copy-start.3 = (bf16[1024,1024]{1,0:T(8,128)(2,1)S(1)}, bf16[1024,1024]{1,0:T(8,128)(2,1)}, u32[]{:S(2)}) copy-start(bf16[1024,1024]{1,0:T(8,128)(2,1)} %get-tuple-element.80) | copy-start | bytes 6291460
  323.1 2.7 copy-start.22
  325.7 2.9 copy-start.14
  372.3 3.2 copy-start.15
  375.7 1.5 copy-start.21
  375.9 9.8 %copy-start.20 = (bf16[4,32,1312]{2,1,0:T(8,128)(2,1)S(1)}, bf16[4,32,1312]{2,1,0:T(8,128)(2,1)}, u32[]{:S(2)}) copy-start(bf16[4,32,1312]{2,1,0:T(8,128)(2,1)} %get-tuple-element.66) | copy-start | bytes 1007620
  386.5 2.0 copy-start.23
  387.0 3.4 copy-start.11

commit v3 on v2

--- a/solution.py
+++ b/solution.py
@@ -460,16 +460,17 @@
             yield from gather_fsdp(links, qkv_all.at[:, f], lambda b: qkv_all.at[:, b])
 
         def out_weights():
+            copies[1].wait()
+            yield from gather_ctx(links, out_ref, lambda b: out_all.at[b, chip, core])
+            mine = out_all.at[:, chip, core]
             far = []
             for k in range(2, fs, 2):
                 slot = links.slot()
-                links.fsdp_copy(slot, out_ref, out_all.at[c, chip, core], f ^ k).start()
+                links.fsdp_copy(slot, mine, mine, f ^ k).start()
                 far.append((slot, k))
             yield
             for slot, k in far:
-                links.fsdp_copy(slot, out_ref, out_all.at[c, (f ^ k) // 2, core], f ^ k).wait()
-            copies[1].wait()
-            yield from gather_ctx(links, out_all.at[c, :, core], lambda b: out_all.at[b, :, core])
+                links.fsdp_copy(slot, mine, out_all.at[:, (f ^ k) // 2, core], f ^ k).wait()
             slot = links.slot()
             links.fsdp_copy(slot, out_all.at[:, :, core], out_all.at[:, :, core], f ^ 1).start()
             yield

time: 397 us -> 389 us (0.980)
  Pallas kernels: 279 us -> 271 us
    pallas_call x8, Pallas kernels: 248 us -> 241 us  [exchange(): pl.pallas_call(kernel, in_specs=[anywhere] * len(operands), out_specs=[an...]
where the time goes in v3:
time: 389 us; the launch traced here: 384 us
  Pallas kernels  271 us (70%)
  local copies, waits for them, and re-layouts  43.8 us (11%)
  other arithmetic  36 us (9%)
  matrix products  30 us (8%)
    pallas_call x8, Pallas kernels, exchange(): pl.pallas_call(kernel, in_specs=[anywhere] * len(operands), out_specs=[an...  241 us
    pallas_call x2, Pallas kernels, grad_blocks(): pl.pallas_call(grad_blocks_kernel, grid_spec=pltpu.PrefetchScalarGridSpec...  10.9 us
    pallas_call x1, Pallas kernels, attend(): pl.pallas_call(lambda *refs: attend_kernel(scale, *refs), grid=(heads, ro...  10 us
    pallas_call x1, Pallas kernels, attend_grads(): pl.pallas_call(lambda *refs: attend_grad_kernel(scale, *refs), grid=(head...  9.57 us
  transfers between devices with their start and end apart: 2, of which 0 were waited for; matrix products, arithmetic and copies ran while one was open for 11% of the time, Pallas kernels for 11%

profile of v3, /device:TPU:11, one launch (start us, length us, event | category | flops | bytes accessed | tf_op | source)
XLA Modules:
  0.0 384.0 jit_solution(5142904078901503812)
XLA Ops:
  2.1 1.0 copy.174
  3.4 1.6 reshape.263
  5.3 1.0 reshape.264.refs_4_
  8.7 85.7 %gather_all.1 = (bf16[8,128,1024]{2,1,0:T(8,128)(2,1)}, f32[8,8,128]{2,1,0:T(8,128)}, bf16[8,4,32,512]{3,2,1,0:T(8,128)(2,1)}, bf16[8,2,2,32,1024]{4,3,2,1,0:T(8...) custom-call(bf16[128,1024]{1,0:T(8,128)(2,1)} %bitcast.153, ...), custom_call_target="tpu_custom_call" | custom-call | tf_op jit(solution)/shard_map/gather_all/pallas_call | solution.py:406
  94.5 1.1 slice_convert_fusion.1
  95.8 1.9 convert_reduce_fusion
  99.7 1.0 fusion.25
  101.6 1.4 slice_bitcast_fusion
  102.9 1.0 copy.133.refs_3_
  105.3 1.1 fusion.40
  106.4 10.0 %attend.1 = (bf16[2,64,1024]{2,1,0:T(8,128)(2,1)}, f32[2,1024,1]{2,1,0:T(8,128)}) custom-call(bf16[2,64,1024]{2,1,0:T(8,128)(2,1)} %get-tuple-element.89.refs_0_, bf16[2,64,1024]{2,1,0:T(8,128)(2,1)} %get-tuple-element.88.refs_1_, bf16[2,64,1024]{2,1,0:T(8,128)(2,1)} %bitcast.167, f32[1024,1]{1,0:T(8,128)} %copy.133.refs_3_, f32[1,1024]{1,0:T(1,128)} %get-tuple-element.98.refs_4_), custom_call_target="tpu_custom_call" | custom-call | tf_op jit(solution)/shard_map/attend/pallas_call | solution.py:139
  116.4 1.8 copy.134
  118.2 7.5 %swap_attended.1 = bf16[8,128,128]{2,1,0:T(8,128)(2,1)} custom-call(bf16[8,128,128]{2,1,0:T(8,128)(2,1)} %bitcast.183), custom_call_target="tpu_custom_call" | custom-call | tf_op jit(solution)/shard_map/swap_attended/pallas_call | solution.py:406
  125.7 2.2 fusion.54
  128.1 0.9 multiply_convert_fusion.4.refs_0_
  129.0 15.1 %gather_normed.1 = bf16[4,128,1024]{2,1,0:T(8,128)(2,1)} custom-call(bf16[128,1024]{1,0:T(8,128)(2,1)} %multiply_convert_fusion.4.refs_0_), custom_call_target="tpu_custom_call" | custom-call | tf_op jit(solution)/shard_map/gather_normed/pallas_call | solution.py:406
  144.1 4.1 %fusion.55 = f32[512,1312]{1,0:T(8,128)S(1)} fusion(bf16[512,1024]{1,0:T(8,128)(2,1)} %bitcast.150, bf16[1024,1312]{1,0:T(8,128)(2,1)} %bitcast.210), kind=kOutput, calls=%fused_computation.139 | convolution fusion | flops 1375731712 | bytes 6422528 | tf_op jit(solution)/shard_map/dot_general | solution.py:722
  148.2 6.0 %multiply_convert_fusion.2 = (bf16[512,656]{1,0:T(8,128)(2,1)}, f32[512,656]{1,0:T(8,128)S(1)}, bf16[512,656]{1,0:T(8,128)(2,1)S(1)}, f32[512,656]{1,0:T(8,128)S(1)}) fusion(f32[512,1312]{1,0:T(8,128)S(1)} %fusion.55, bf16[512,1024]{1,0:T(8,128)(2,1)S(1)} %bitcast.165, bf16[1024,656]{1,0:T(8,128)(2,1)S(1)} %bitcast.212), kind=kOutput, calls=%fused_computation.25 | convolution fusion | flops 713728000 | bytes 9109504 | tf_op jit(solution)/shard_map/td,df->tf/dot_general | solution.py:727
  154.4 1.6 pad_maximum_fusion.refs_1_
  156.0 5.3 %grad_blocks.2 = (bf16[4,128,1312]{2,1,0:T(8,128)(2,1)}, bf16[4,128,656]{2,1,0:T(8,128)(2,1)}) custom-call(s32[1]{0:T(128)S(6)} %sub.64.side_ref, bf16[512,1024]{1,0:T(8,128)(2,1)} %bitcast.151, bf16[512,1312]{1,0:T(8,128)(2,1)} %pad_maximum_fusion.refs_1_, bf16[512,1024]{1,0:T(8,128)(2,1)} %bitcast.163, bf16[512,656]{1,0:T(8,128)(2,1)} %get-tuple-element.75.refs_3_), custom_call_target="tpu_custom_call" | custom-call | flops 1031798784 | bytes 3145728 | tf_op jit(solution)/shard_map/grad_blocks/pallas_call | solution.py:610
  161.2 2.5 copy.148
  164.4 2.2 copy.149
  166.6 0.8 collective-permute-start.1
  167.5 5.1 %convolution_convert_fusion.1 = bf16[512,1024]{1,0:T(8,128)(2,1)} fusion(bf16[512,1312]{1,0:T(8,128)(2,1)} %pad_maximum_fusion.refs_1_, bf16[1024,1312]{1,0:T(8,128)(2,1)} %bitcast.211), kind=kOutput, calls=%fused_computation.43 | convolution fusion | flops 1376256000 | bytes 5079040 | tf_op jit(solution)/shard_map/tf,df->td/dot_general | solution.py:731
  172.5 15.0 %swap_grad_normed.1 = bf16[4,128,1024]{2,1,0:T(8,128)(2,1)} custom-call(bf16[4,128,1024]{2,1,0:T(8,128)(2,1)} %bitcast.179), custom_call_target="tpu_custom_call" | custom-call | tf_op jit(solution)/shard_map/swap_grad_normed/pallas_call | solution.py:406
  187.5 1.5 convert_reduce_fusion.3
  189.3 1.1 fusion.49
  190.8 1.5 convolution_convert_fusion.3
  192.3 0.8 copy.142
  194.0 1.1 copy.140
  195.2 0.8 copy.141
  196.0 0.9 copy.143
  196.9 19.1 %swap_grad_attended.1 = (bf16[8,128,128]{2,1,0:T(8,128)(2,1)}, bf16[4,128,256]{2,1,0:T(8,128)(2,1)}, bf16[4,128,1024]{2,1,0:T(8,128)(2,1)}) custom-call(bf16[8,128,128]{2,1,0:T(8,128)(2,1)} %bitcast.174, bf16[4,128,256]{2,1,0:T(8,128)(2,1)} %bitcast.175, bf16[128,1024]{1,0:T(8,128)(2,1)} %copy_bitcast_fusion.2.refs_2_), custom_call_target="tpu_custom_call" | custom-call | tf_op jit(solution)/shard_map/swap_grad_attended/pallas_call | solution.py:406
  216.0 1.8 copy.144
  217.8 9.6 %attend_grads.1 = (f32[2,64,1024]{2,1,0:T(8,128)}, f32[2,64,1024]{2,1,0:T(8,128)}, f32[2,64,1024]{2,1,0:T(8,128)}) custom-call(bf16[2,64,1024]{2,1,0:T(8,128)(2,1)} %get-tuple-element.89.refs_0_, bf16[2,64,1024]{2,1,0:T(8,128)(2,1)} %get-tuple-element.88.refs_1_, bf16[2,64,1024]{2,1,0:T(8,128)(2,1)} %bitcast.168, f32[1024,1]{1,0:T(8,128)} %copy.133.refs_3_, ...), custom_call_target="tpu_custom_call" | custom-call | tf_op jit(solution)/shard_map/attend_grads/pallas_call | solution.py:159
  227.3 1.3 broadcast_multiply_fusion.1
  228.8 0.8 copy-done.9
  230.3 1.4 copy-done.26
  231.7 3.0 multiply_reduce_fusion
  234.7 2.3 copy.146
  236.9 1.7 convolution_convert_fusion.2
  238.6 0.8 copy.156.refs_1_
  239.5 2.0 multiply_convert_fusion
  241.5 2.9 copy.152
  244.6 3.3 fusion.19
  248.2 2.4 maximum_bitcast_fusion.refs_4_
  250.6 2.0 convolution_convert_fusion
  252.6 2.2 copy.151.refs_5_
  254.9 2.5 copy.150.refs_4_
  257.4 5.7 %grad_blocks.3 = (bf16[4,128,1312]{2,1,0:T(8,128)(2,1)}, bf16[4,128,656]{2,1,0:T(8,128)(2,1)}) custom-call(s32[1]{0:T(128)} %bitcast.47.side_ref, bf16[512,1024]{1,0:T(8,128)(2,1)} %bitcast.152, bf16[512,1312]{1,0:T(8,128)(2,1)} %pad_maximum_fusion.refs_1_, bf16[512,1024]{1,0:T(8,128)(2,1)} %bitcast.164, bf16[512,656]{1,0:T(8,128)(2,1)} %get-tuple-element.75.refs_3_, ...), custom_call_target="tpu_custom_call" | custom-call | flops 1031798784 | bytes 3145728 | tf_op jit(solution)/shard_map/grad_blocks/pallas_call | solution.py:610
  263.1 53.0 %pair_stage.1 = (bf16[4,128,1024]{2,1,0:T(8,128)(2,1)}, bf16[4,128,256]{2,1,0:T(8,128)(2,1)}, bf16[4,128,1312]{2,1,0:T(8,128)(2,1)}, bf16[4,128,656]{2,1,0:T(8,1...) custom-call(bf16[4,2,128,1024]{3,2,1,0:T(8,128)(2,1)} %bitcast.157, ...), custom_call_target="tpu_custom_call" | custom-call | tf_op jit(solution)/shard_map/pair_stage/pallas_call | solution.py:406
  316.1 2.7 fusion.1.refs_0_
  319.5 2.2 reduce_sum.204.refs_2_
  321.7 1.0 reduce_sum.205
  322.7 2.0 reduce_sum.206
  324.7 39.5 %line_stage.1 = (bf16[4,128,1024]{2,1,0:T(8,128)(2,1)}, bf16[4,128,256]{2,1,0:T(8,128)(2,1)}, bf16[8,32,512]{2,1,0:T(8,128)(2,1)}, bf16[4,32,1312]{2,1,0:T(8,128)(2,1)}, bf16[4,32,656]{2,1,0:T(8,128)(2,1)}) custom-call(bf16[4,128,1024]{2,1,0:T(8,128)(2,1)} %fusion.1.refs_0_, bf16[4,128,256]{2,1,0:T(8,128)(2,1)} %fusion.43.refs_1_, ...), custom_call_target="tpu_custom_call" | custom-call | tf_op jit(solution)/shard_map/line_stage/pallas_call | solution.py:406
  364.2 1.0 slice_convert_fusion.2
  365.2 0.9 convert_reduce_fusion.5
  366.2 1.5 convert_reduce_fusion.2
  370.8 6.1 %swap_weight_grads.1 = bf16[4,32,256]{2,1,0:T(8,128)(2,1)} custom-call(bf16[4,32,256]{2,1,0:T(8,128)(2,1)} %bitcast.195), custom_call_target="tpu_custom_call" | custom-call | tf_op jit(solution)/shard_map/swap_weight_grads/pallas_call | solution.py:406
  376.8 0.9 convert_bitcast_fusion.1
  379.7 1.4 reshape.305
  381.4 1.0 reshape.307
  383.1 1.0 fusion.45
  (121 shorter events, 19.3 us)
Async XLA Ops:
  3.1 3.3 copy-start.24
  94.5 3.3 copy-start
  98.5 1.2 copy-start.25
  104.6 0.7 copy-start.6
  104.6 1.8 copy-start.8
  106.4 19.3 %copy-start.1 = (bf16[1,128,1024]{2,1,0:T(8,128)(2,1)S(1)}, bf16[1,128,1024]{2,1,0:T(8,128)(2,1)}, u32[]{:S(2)}) copy-start(bf16[1,128,1024]{2,1,0:T(8,128)(2,1)} %param.9) | copy-start | bytes 786436
  144.1 4.1 %copy-start.4 = (bf16[4,128,1024]{2,1,0:T(8,128)(2,1)S(1)}, bf16[4,128,1024]{2,1,0:T(8,128)(2,1)}, u32[]{:S(2)}) copy-start(bf16[4,128,1024]{2,1,0:T(8,128)(2,1)} %get-tuple-element.44) | copy-start | bytes 3145732
  144.1 4.1 %copy-start.27 = (bf16[8,4,32,656]{3,2,1,0:T(8,128)(2,1)S(1)}, bf16[8,4,32,656]{3,2,1,0:T(8,128)(2,1)}, u32[]{:S(2)}) copy-start(bf16[8,4,32,656]{3,2,1,0:T(8,128)(2,1)} %get-tuple-element.45) | copy-start | bytes 4030468
  163.7 91.1 %collective-permute-start = (bf16[4,128,1312]{1,2,0:T(8,128)(2,1)}, bf16[4,128,1312]{1,2,0:T(8,128)(2,1)}, u32[]{:S(2)}, u32[]{:S(2)}) collective-permute-start(bf16[4,128,1312]{1,2,0:T(8,128)(2,1)} %copy.148), channel_id=1, source_target_pairs={{0,4},{4,0},{8,12},{12,8},{16,20},{20,16},{24,28},{28,24},{1,5},{5... | collective-permute-start | bytes 4030472 | tf_op jit(solution)/shard_map/ppermute | solution.py:748
  166.6 86.0 %collective-permute-start.1 = (bf16[4,128,656]{1,2,0:T(8,128)(2,1)}, bf16[4,128,656]{1,2,0:T(8,128)(2,1)}, u32[]{:S(2)}, u32[]{:S(2)}) collective-permute-start(bf16[4,128,656]{1,2,0:T(8,128)(2,1)} %copy.149), channel_id=1, source_target_pairs={{0,4},{4,0},{8,12},{12,8},{16,20},{20,16},{24,28},{28,24},{1,5},{5... | collective-permute-start | bytes 2015240 | tf_op jit(solution)/shard_map/ppermute | solution.py:748
  187.5 1.8 copy-start.16
  189.0 1.8 copy-start.2
  190.8 2.4 copy-start.10
  193.2 2.8 copy-start.17
  217.8 9.6 %copy-start.7 = (f32[64,1024]{1,0:T(8,128)S(1)}, f32[64,1024]{1,0:T(8,128)}, u32[]{:S(2)}) copy-start(f32[64,1024]{1,0:T(8,128)} %copy-done.6) | copy-start | bytes 786436
  228.6 1.0 copy-start.9
  228.6 1.1 copy-start.12
  228.7 1.3 copy-start.13
  228.8 1.4 copy-start.19
  230.1 1.5 copy-start.26
  230.3 4.4 %copy-start.18 = (bf16[3,2,64,1024]{3,2,1,0:T(8,128)(2,1)}, bf16[3,2,64,1024]{3,2,1,0:T(8,128)(2,1)S(1)}, u32[]{:S(2)}) copy-start(bf16[3,2,64,1024]{3,2,1,0:T(8,128)(2,1)S(1)} %maximum_convert_fusion) | copy-start | bytes 2359300
  247.9 2.7 copy-start.5
  248.2 2.4 copy-start.28
  263.1 53.0 %copy-start.3 = (bf16[1024,1024]{1,0:T(8,128)(2,1)S(1)}, bf16[1024,1024]{1,0:T(8,128)(2,1)}, u32[]{:S(2)}) copy-start(bf16[1024,1024]{1,0:T(8,128)(2,1)} %get-tuple-element.80) | copy-start | bytes 6291460
  316.1 2.7 copy-start.22
  318.7 2.9 copy-start.14
  365.2 3.2 copy-start.15
  368.6 1.5 copy-start.21
  368.8 9.5 %copy-start.20 = (bf16[4,32,1312]{2,1,0:T(8,128)(2,1)S(1)}, bf16[4,32,1312]{2,1,0:T(8,128)(2,1)}, u32[]{:S(2)}) copy-start(bf16[4,32,1312]{2,1,0:T(8,128)(2,1)} %get-tuple-element.66) | copy-start | bytes 1007620
  379.1 2.0 copy-start.23
  379.6 3.4 copy-start.11
